TPU v7x, 512 devices: a whole 4x8x8 slice. The times are simulated.
512 devices in a mesh: agg: 32 (over x, y), grp: 16 (over z, core).
Axes of the slice: x: 4, y: 8, z: 8, core: 2. Of those that a mesh axis runs over, the one named last changes fastest.
Arguments:
- a_blocks: bfloat16 [32, 16, 16, 5, 128, 128], P('agg', 'grp'), may hold values from -0.5 to 0.5
- a_cols: int32 [32, 16, 16, 5], P('agg', 'grp'), may hold values from 0 to 23, as said below
- p_blocks: bfloat16 [32, 16, 16, 2, 128, 128], P('agg', 'grp'), may hold values from -0.5 to 0.5
- p_cols: int32 [32, 16, 16, 2], P(None, 'grp'), may hold values from 0 to 2, as said below
Outputs:
- coarse_matrix: bfloat16 [32, 128, 3, 9, 128], P('agg')
Inputs may be any that keep to these rules, and one draw needn't show every extreme that they name: `a_cols`: slot 0 of row r is 4 + r. In every region but the first, slot 1 of the rows r < 4 names a row 0 to 4 - 1 (row 0 names 0); in every region but the last, slot 4 of the rows r >= 12 names a row 20 to 16 + 2 * 4 - 1 (row 15 names the last). All other slots name rows 4 to 19; a row may name a column more than once. `p_cols`: the 2 entries of a row are 2 consecutive coarse rows counted modulo 3, all different. Every index of agg holds the whole array.
All inputs are finite; a program needn't handle non-finite values.
Results may differ from a plain program's by a relative error of at most 0.025.
Values may be sent and summed in bfloat16 or wider, within the bound.
No kernel may reach another device: no remote copies, remote signals or barrier semaphores. Data moves between devices by JAX's collectives and lax.ppermute only.
A program may use at most 64 MiB of HBM per device.

v0:
```python
import jax
import jax.numpy as jnp
from jax import lax
from jax.sharding import PartitionSpec as P

NC = 3
HB = 4


def with_halo(block, sides, width):
    for axis, dim in sides:
        count = lax.axis_size(axis)
        forward = [(i, i + 1) for i in range(count - 1)]
        backward = [(target, source) for source, target in forward]
        low = lax.ppermute(
            lax.slice_in_dim(block, block.shape[dim] - width, None, axis=dim), axis, forward
        )
        high = lax.ppermute(lax.slice_in_dim(block, 0, width, axis=dim), axis, backward)
        block = jnp.concatenate([low, block, high], axis=dim)
    return block


def body(a_blocks, a_cols, p_blocks, p_cols):
    a_local = a_blocks[0, 0]
    col_local = a_cols[0, 0]
    p_local = p_blocks[0, 0]
    row_count, a_slots = col_local.shape
    p_slots = p_local.shape[1]
    width = p_local.shape[-1]
    band = 3 * NC
    group_rows = 4
    group_count = row_count // group_rows
    region = lax.axis_index("agg")
    last_region = lax.axis_size("agg") - 1
    p_extended = with_halo(p_local, (("agg", 0),), HB)
    pattern = p_cols[:, 0]

    def region_ids(index):
        return lax.dynamic_index_in_dim(pattern, index, 0, keepdims=False)

    pattern_own = region_ids(region)
    ids_extended = jnp.concatenate(
        [
            region_ids(jnp.maximum(region - 1, 0))[row_count - HB :],
            pattern_own + NC,
            region_ids(jnp.minimum(region + 1, last_region))[:HB] + 2 * NC,
        ],
        0,
    )
    slot_ids = ids_extended[col_local].reshape(row_count, a_slots * p_slots)

    def product_group(inputs):
        a_group, col_group = inputs
        taken = p_extended[col_group]
        result = jnp.einsum("rkxy,rkmyz->rkmxz", a_group, taken, preferred_element_type=jnp.float32)
        return result.astype(jnp.bfloat16).reshape(group_rows, a_slots * p_slots, width, width)

    applied = lax.map(
        product_group,
        (
            a_local.reshape(group_count, group_rows, a_slots, width, width),
            col_local.reshape(group_count, group_rows, a_slots),
        ),
    )
    applied = applied.reshape(row_count, a_slots * p_slots, width, width)
    band_mask = (slot_ids[:, :, None] == jnp.arange(band, dtype=jnp.int32)[None, None, :]).astype(
        jnp.bfloat16
    )
    grouped = jnp.einsum("rsd,rsxz->rdxz", band_mask, applied, preferred_element_type=jnp.float32)
    grouped_high = grouped.astype(jnp.bfloat16)
    grouped_low = (grouped - grouped_high.astype(jnp.float32)).astype(jnp.bfloat16)
    coarse_mask = (
        pattern_own[:, :, None] == jnp.arange(NC, dtype=jnp.int32)[None, None, :]
    ).astype(jnp.bfloat16)
    p_routed = jnp.einsum(
        "rnc,rnxy->rcxy", coarse_mask, p_local, preferred_element_type=jnp.float32
    ).astype(jnp.bfloat16)
    term = jnp.einsum("rcxy,rdxz->ycdz", p_routed, grouped_high, preferred_element_type=jnp.float32)
    term = term + jnp.einsum(
        "rcxy,rdxz->ycdz", p_routed, grouped_low, preferred_element_type=jnp.float32
    )
    summed = lax.psum(term.astype(jnp.bfloat16), "grp")
    return summed.reshape(1, width, NC, band, width)


def solution(mesh):
    return jax.shard_map(
        body,
        mesh=mesh,
        in_specs=(
            P("agg", "grp", None, None, None, None),
            P("agg", "grp", None, None),
            P("agg", "grp", None, None, None, None),
            P(None, "grp", None, None),
        ),
        out_specs=P("agg", None, None, None, None),
        check_vma=False,
    )
```

profile of v0, /device:TPU:7, one launch (start us, length us, event | category | flops | bytes accessed | tf_op | source)
XLA Modules:
  0.0 200.4 jit_solution(4998686334016627752)
XLA Ops:
  6.5 0.0 all-reduce.2.cloned.1.call-start
  6.5 1.1 slice_bitcast_fusion.1
  7.6 3.2 %collective-permute-start = (bf16[4,2,128,128]{3,2,1,0:T(8,128)(2,1)S(1)}, bf16[4,2,128,128]{3,2,1,0:T(8,128)(2,1)S(1)}, u32[]{:S(2)}, u32[]{:S(2)}) collective-permute-start(bf16[4,2,128,128]{3,2,1,0:T(8,128)(2,1)S(1)} %get-tuple-element.63), channel_id=1, source_target_pairs={{0,16},{16,32},{32,48},{48,64},{64,80},{80,96},{96,112},{112,128},... | collective-permute-start | bytes 786440 | tf_op jit(solution)/shard_map/ppermute | solution.py:15
  10.8 4.2 %collective-permute-start.1 = (bf16[4,2,128,128]{3,2,1,0:T(8,128)(2,1)S(1)}, bf16[4,2,128,128]{3,2,1,0:T(8,128)(2,1)S(1)}, u32[]{:S(2)}, u32[]{:S(2)}) collective-permute-start(bf16[4,2,128,128]{3,2,1,0:T(8,128)(2,1)S(1)} %get-tuple-element.64), channel_id=1, source_target_pairs={{16,0},{32,16},{48,32},{64,48},{80,64},{96,80},{112,96},{128,112},... | collective-permute-start | bytes 786440 | tf_op jit(solution)/shard_map/ppermute | solution.py:18
  15.0 0.7 compare_select_fusion.1
  15.7 0.8 copy.80
  16.5 0.8 constant_dynamic-slice_fusion.2
  17.3 0.1 copy.86
  17.4 0.1 copy.55
  17.5 0.8 constant_dynamic-slice_fusion.1
  18.3 0.1 copy.56
  18.4 0.1 pad_add_fusion
  18.4 0.1 copy.59
  18.5 0.1 copy.58
  18.6 0.1 reshape.91
  18.7 0.6 gather_fusion.1
  19.3 0.1 eq.28
  19.4 0.1 copy.63
  19.5 0.0 copy-start
  19.5 4.4 %fusion.23 = bf16[16,3,128,128]{3,1,2,0:T(4,128)(2,1)} fusion(bf16[16,2,128,128]{3,2,1,0:T(8,128)(2,1)} %bitcast.91, s32[16,2]{1,0:T(8,128)S(1)} %copy.63), kind=kOutput, calls=%fused_computation.26 | convolution fusion | flops 3145824 | bytes 2621568 | tf_op jit(solution)/shard_map/rnc,rnxy->rcxy/dot_general | solution.py:75
  23.9 0.0 collective-permute-done
  23.9 0.0 collective-permute-done.1
  23.9 0.0 copy-done
  23.9 0.2 pad_maximum_fusion
  24.1 15.0 %while.10 = (s32[]{:T(128)}, bf16[4,4,10,128,128]{3,4,2,1,0:T(8,128)(2,1)}, s32[4,4,5]{2,1,0:T(4,128)S(1)}, bf16[24,2,128,128]{3,2,1,0:T(8,128)(2,1)S(1)}, bf16[4,4,5,128,128]{4,3,2,1,0:T(8,128)(2,1)}, /*index=5*/s32[]{:T(128)}) while((s32[]{:T(128)}, bf16[4,4,10,128,128]{3,4,2,1,0:T(8,128)(2,1)}, s32[4,4,5]{2,1,0:T(4,128)S(1)}, ...), condition=%wide.region_1.2_spmd, body=%wide.region_0.1_spmd.sunk | while | flops 168428608 | bytes 8525353 | solution.py:58
  24.1 0.1 reshape.114
  24.2 0.8 gather_fusion
  25.0 1.6 convolution_convert_fusion.2
  26.7 1.2 constant_dynamic-update-slice_fusion.2
  27.9 0.1 reshape.114
  28.0 0.8 gather_fusion
  28.8 1.6 convolution_convert_fusion.2
  30.5 1.2 constant_dynamic-update-slice_fusion.2
  31.6 0.1 reshape.114
  31.7 0.8 gather_fusion
  32.5 1.6 convolution_convert_fusion.2
  34.2 1.1 constant_dynamic-update-slice_fusion.2
  35.3 0.1 reshape.114
  35.4 0.8 gather_fusion
  36.2 1.6 convolution_convert_fusion.2
  37.9 1.2 constant_dynamic-update-slice_fusion.2
  39.1 12.7 %copy.61 = bf16[16,10,128,128]{3,1,2,0:T(8,128)(2,1)} copy(bf16[16,10,128,128]{2,3,1,0:T(8,128)(2,1)} %bitcast.89) | data formatting | bytes 10485760 | tf_op jit(solution)/shard_map/reshape | solution.py:65
  51.8 0.0 copy-start.1
  51.8 5.8 %fusion.26 = f32[16,9,128,128]{3,1,2,0:T(8,128)S(1)} fusion(bf16[16,10,128,128]{3,1,2,0:T(8,128)(2,1)} %copy.61, s32[16,10]{1,0:T(8,128)S(1)} %eq.28), kind=kOutput, calls=%fused_computation.32 | convolution fusion | flops 47187360 | bytes 14680704 | tf_op jit(solution)/shard_map/rsd,rsxz->rdxz/dot_general | solution.py:69
  57.7 0.0 copy-done.1
  57.7 5.0 %fusion.5 = f32[9,128,3,128,1]{3,1,4,2,0:T(8,128)S(1)} fusion(f32[16,9,128,128]{3,1,2,0:T(8,128)S(1)} %fusion.26, bf16[16,3,128,128]{3,1,2,0:T(4,128)(2,1)S(1)} %copy-done.1), kind=kOutput, calls=%fused_computation.13 | convolution fusion | flops 1821376512 | bytes 12779520 | tf_op jit(solution)/shard_map/rcxy,rdxz->ycdz/dot_general | solution.py:79
  62.7 7.0 %fusion.18 = bf16[1,128,3,9,128]{1,4,2,3,0:T(8,128)(2,1)} fusion(f32[9,128,3,128,1]{3,1,4,2,0:T(8,128)S(1)} %fusion.5, f32[16,9,128,128]{3,1,2,0:T(8,128)S(1)} %fusion.26, bf16[16,3,128,128]{3,1,2,0:T(4,128)(2,1)S(1)} %copy-done.1), kind=kOutput, calls=%fused_computation.25 | convolution fusion | flops 1812824064 | bytes 13664256 | tf_op jit(solution)/shard_map/rcxy,rdxz->ycdz/dot_general | solution.py:78
  69.7 0.0 all-reduce.2.cloned.1.call-update
  69.7 121.6 %all-reduce.2.cloned.1.call-done = bf16[1,128,3,9,128]{1,4,2,3,0:T(8,128)(2,1)} async-done(((bf16[1,128,3,9,128]{1,4,2,3,0:T(8,128)(2,1)}), bf16[1,128,3,9,128]{1,4,2,3,0:T(8,128)(2,1)}) %all-reduce.2.cloned.1.call-update) | async-done | bytes 884752 | tf_op jit(solution)/shard_map/psum | solution.py:82
  191.4 2.2 %copy.71 = bf16[1,128,3,9,128]{4,1,3,2,0:T(8,128)(2,1)} copy(bf16[1,128,3,9,128]{1,4,2,3,0:T(8,128)(2,1)} %all-reduce.2.cloned.1.call-done) | data formatting | bytes 1769472 | tf_op jit(solution)/shard_map/psum | solution.py:82
  (12 shorter events, 0.1 us)
Async XLA Ops:
  6.5 184.8 %all-reduce.2.cloned.1.call-start = ((), (), s32[]{:S(2)}) async-start(), calls=%async_computation | async-start | bytes 1769472 | tf_op jit(solution)/shard_map/psum | solution.py:82
  7.6 16.3 %collective-permute-start = (bf16[4,2,128,128]{3,2,1,0:T(8,128)(2,1)S(1)}, bf16[4,2,128,128]{3,2,1,0:T(8,128)(2,1)S(1)}, u32[]{:S(2)}, u32[]{:S(2)}) collective-permute-start(bf16[4,2,128,128]{3,2,1,0:T(8,128)(2,1)S(1)} %get-tuple-element.63), channel_id=1, source_target_pairs={{0,16},{16,32},{32,48},{48,64},{64,80},{80,96},{96,112},{112,128},... | collective-permute-start | bytes 786440 | tf_op jit(solution)/shard_map/ppermute | solution.py:15
  10.8 13.1 %collective-permute-start.1 = (bf16[4,2,128,128]{3,2,1,0:T(8,128)(2,1)S(1)}, bf16[4,2,128,128]{3,2,1,0:T(8,128)(2,1)S(1)}, u32[]{:S(2)}, u32[]{:S(2)}) collective-permute-start(bf16[4,2,128,128]{3,2,1,0:T(8,128)(2,1)S(1)} %get-tuple-element.64), channel_id=1, source_target_pairs={{16,0},{32,16},{48,32},{64,48},{80,64},{96,80},{112,96},{128,112},... | collective-permute-start | bytes 786440 | tf_op jit(solution)/shard_map/ppermute | solution.py:18
  19.5 4.4 %copy-start = (bf16[1,1,16,2,128,128]{5,4,3,2,1,0:T(8,128)(2,1)S(1)}, bf16[1,1,16,2,128,128]{5,4,3,2,1,0:T(8,128)(2,1)}, u32[]{:S(2)}) copy-start(bf16[1,1,16,2,128,128]{5,4,3,2,1,0:T(8,128)(2,1)} %param.8) | copy-start | bytes 3145732
  51.8 5.8 %copy-start.1 = (bf16[16,3,128,128]{3,1,2,0:T(4,128)(2,1)S(1)}, bf16[16,3,128,128]{3,1,2,0:T(4,128)(2,1)}, u32[]{:S(2)}) copy-start(bf16[16,3,128,128]{3,1,2,0:T(4,128)(2,1)} %fusion.23) | copy-start | bytes 4718596
Sparse Core Ops, SparseCore 0:
  69.9 121.4 all-reduce.1
where the time goes:
time: 202 us; the launch traced here: 200 us
  waiting for transfers between devices  122 us (60%)
  matrix products  28.8 us (14%)
  local copies, waits for them, and re-layouts  28 us (14%)
  between operations  13.5 us (7%)
  starting transfers between devices  7.39 us (4%)
    psum x1, waiting for transfers between devices, body(): summed = lax.psum(term.astype(jnp.bfloat16), 'grp')  122 us
    reshape x1, local copies, waits for them, and re-layouts, body(): applied = applied.reshape(row_count, a_slots * p_slots, width, width)  12.7 us
    dot_general x1, matrix products, body(): jnp.einsum('rcxy,rdxz->ycdz', p_routed, grouped_high, preferred_element_t...  7.05 us
    dot_general x4, matrix products, product_group(): jnp.einsum('rkxy,rkmyz->rkmxz', a_group, taken, preferred_element_type=jn...  6.56 us
    dot_general x1, matrix products, body(): jnp.einsum('rsd,rsxz->rdxz', band_mask, applied, preferred_element_type=j...  5.84 us
    dot_general x1, matrix products, body(): jnp.einsum('rcxy,rdxz->ycdz', p_routed, grouped_low, preferred_element_ty...  4.99 us
    dynamic_update_slice x4, local copies, waits for them, and re-layouts, body(): lax.map(product_group, (a_local.reshape(group_count, group_rows, a_slots,...  4.75 us
    dot_general x1, matrix products, body(): jnp.einsum('rnc,rnxy->rcxy', coarse_mask, p_local, preferred_element_type...  4.39 us
  transfers between devices with their start and end apart: 3, of which 1 were waited for; matrix products, arithmetic and copies ran while one was open for 4% of the time, Pallas kernels for 0%

commit v1 on v0

v1 whole, which is shorter than its diff:
```python
import functools

import jax
import jax.numpy as jnp
from jax import lax
from jax.experimental import pallas as pl
from jax.experimental.pallas import tpu as pltpu
from jax.sharding import Mesh
from jax.sharding import PartitionSpec as P

NC = 3
HB = 4
F32 = jnp.float32
BF16 = jnp.bfloat16


def contract_rows(a, b):
    return lax.dot_general(a, b, (((0,), (0,)), ((), ())), preferred_element_type=F32)


def own_kernel(fr, ka, b, acol, pcol, a, p, own, w_lo, w_hi, routed, grouped):
    region = lax.axis_index("agg")
    zeros = jnp.zeros((b, b), BF16)
    for d in range(NC):
        routed[d, pl.ds(fr * b, b), :] = zeros
    for r in range(fr):
        first, second = pcol[2 * r, region], pcol[2 * r + 1, region]
        rows = pl.ds(r * b, b)
        routed[first, rows, :] = p[r, 0]
        routed[second, rows, :] = p[r, 1]
        routed[NC - first - second, rows, :] = zeros

    def block_row(start):
        rows = pl.ds(pl.multiple_of(start, b), b)
        return jnp.concatenate([routed[d, rows, :] for d in range(NC)], axis=1)

    for r in range(fr):
        starts = []
        for k in range(ka):
            col = acol[k, r]
            own_row = (col >= HB) & (col < HB + fr)
            starts.append(jnp.where(own_row, col - HB, fr) * b)
        left = jnp.concatenate([a[r, k] for k in range(ka)], axis=1)
        right = jnp.concatenate([block_row(s) for s in starts], axis=0)
        g = jnp.dot(left, right, preferred_element_type=F32)
        grouped[pl.ds(r * b, b), :] = g.astype(BF16)
    every = jnp.concatenate([routed[d, pl.ds(0, fr * b), :] for d in range(NC)], axis=1)
    own[...] = contract_rows(every, grouped[...]).astype(BF16)

    for out, first_row, slot, least in ((w_lo, 0, 1, None), (w_hi, fr - HB, ka - 1, HB + fr)):
        for i in range(HB):
            r = first_row + i
            col = acol[slot, r]
            outside = col < HB if least is None else col >= least
            w = contract_rows(block_row(r * b), a[r, slot])
            out[:, pl.ds(i * b, b)] = jnp.where(outside, w, 0.0).astype(BF16)


def halo_kernel(fr, ka, b, pieces, regions, acol, pcol, own, w_lo, w_hi, lo, hi, keep, send, routed):
    region = lax.axis_index("agg")
    core = lax.axis_index("core")
    zeros = jnp.zeros((b, b), BF16)
    band = 3 * NC
    per = NC * band * b // pieces

    def halo_part(w, halo, first_row, slot, base, source, source_row):
        for i in range(HB):
            j = jnp.clip(acol[slot, first_row + i] - base, 0, HB - 1)
            at = 2 * (source_row + j)
            first, second = pcol[at, source], pcol[at + 1, source]
            rows = pl.ds(i * b, b)
            routed[first, rows, :] = halo[j, 0]
            routed[second, rows, :] = halo[j, 1]
            routed[NC - first - second, rows, :] = zeros
        right = jnp.concatenate([routed[d] for d in range(NC)], axis=1)
        return jnp.dot(w[...], right, preferred_element_type=F32).astype(BF16)

    parts = [
        halo_part(w_lo, lo, 0, 1, 0, jnp.maximum(region - 1, 0), fr - HB),
        own[...],
        halo_part(w_hi, hi, fr - HB, ka - 1, HB + fr, jnp.minimum(region + 1, regions - 1), 0),
    ]

    def write(even, odd):
        for c in range(NC):
            for d in range(band):
                block = parts[d // NC][c * b : (c + 1) * b, (d % NC) * b : (d % NC + 1) * b]
                at = (c * band + d) * b
                done = 0
                while done < b:
                    q, offset = divmod(at + done, per)
                    count = min(b - done, per - offset)
                    (even, odd)[q % 2][q // 2, offset : offset + count, :] = block[done : done + count]
                    done += count

    @pl.when(core == 0)
    def _():
        write(keep, send)

    @pl.when(core == 1)
    def _():
        write(send, keep)


def body(a_blocks, a_cols, p_blocks, p_cols):
    a_local, p_local = a_blocks[0, 0], p_blocks[0, 0]
    fr, ka, b = a_local.shape[:3]
    regions = p_cols.shape[0]
    acol = a_cols[0, 0].T
    pcol = p_cols[:, 0].transpose(1, 2, 0).reshape(fr * 2, regions)
    band = 3 * NC
    z_count, core_count = lax.axis_size("z"), lax.axis_size("core")
    pieces = z_count * core_count
    per = NC * band * b // pieces
    forward = [(i, i + 1) for i in range(regions - 1)]
    backward = [(target, source) for source, target in forward]
    lo = lax.ppermute(p_local[fr - HB :], "agg", forward)
    hi = lax.ppermute(p_local[:HB], "agg", backward)

    vmem = pl.BlockSpec(memory_space=pltpu.VMEM)
    smem = pl.BlockSpec(memory_space=pltpu.SMEM)
    n = NC * b
    own, w_lo, w_hi = pl.pallas_call(
        functools.partial(own_kernel, fr, ka, b),
        out_shape=[
            jax.ShapeDtypeStruct((n, n), BF16),
            jax.ShapeDtypeStruct((n, HB * b), BF16),
            jax.ShapeDtypeStruct((n, HB * b), BF16),
        ],
        in_specs=[smem, smem, vmem, vmem],
        out_specs=[vmem] * 3,
        scratch_shapes=[
            pltpu.VMEM((NC, (fr + 1) * b, b), BF16),
            pltpu.VMEM((fr * b, n), BF16),
        ],
        cost_estimate=pl.CostEstimate(flops=2_000_000_000, bytes_accessed=6_000_000, transcendentals=0),
        compiler_params=pltpu.CompilerParams(vmem_limit_bytes=40 << 20),
        name="own_part",
    )(acol, pcol, a_local, p_local)

    keep, send = pl.pallas_call(
        functools.partial(halo_kernel, fr, ka, b, pieces, regions),
        out_shape=[jax.ShapeDtypeStruct((z_count, per, b), BF16)] * 2,
        in_specs=[smem, smem] + [vmem] * 5,
        out_specs=[vmem] * 2,
        scratch_shapes=[pltpu.VMEM((NC, HB * b, b), BF16)],
        cost_estimate=pl.CostEstimate(flops=400_000_000, bytes_accessed=3_000_000, transcendentals=0),
        compiler_params=pltpu.CompilerParams(vmem_limit_bytes=20 << 20),
        name="halo_part",
    )(acol, pcol, own, w_lo, w_hi, lo, hi)

    got = lax.ppermute(send, "core", [(0, 1), (1, 0)])
    pair = (keep.astype(F32) + got.astype(F32)).astype(BF16)
    mine = lax.all_to_all(pair, "z", 0, 0, tiled=True)
    mine = mine.astype(F32).sum(0).astype(BF16)
    whole = lax.all_gather(mine, ("z", "core"), tiled=True)
    return whole.reshape(NC, band, b, b).transpose(2, 0, 1, 3)[None]


def solution(mesh):
    agg, grp = mesh.devices.shape
    split = Mesh(mesh.devices.reshape(agg, grp // 2, 2), ("agg", "z", "core"))
    both = ("z", "core")
    return jax.shard_map(
        body,
        mesh=split,
        in_specs=(
            P("agg", both, None, None, None, None),
            P("agg", both, None, None),
            P("agg", both, None, None, None, None),
            P(None, both, None, None),
        ),
        out_specs=P("agg", None, None, None, None),
        check_vma=False,
    )
```

time: 202 us -> 69.1 us (0.34)
  waiting for transfers between devices: 122 us -> 2.11 us
  blocking collectives: 0 us -> 43.5 us
  matrix products: 28.8 us -> 0 us
  local copies, waits for them, and re-layouts: 28 us -> 6.34 us
  between operations: 13.5 us -> 0.07 us
  Pallas kernels: 0 us -> 5.44 us
  starting transfers between devices: 7.39 us -> 11.1 us
    psum x1 -> x0, waiting for transfers between devices: 122 us -> none  [body(): summed = lax.psum(term.astype(jnp.bfloat16), 'grp')]
    dot_general x8 -> x0, matrix products: 28.8 us -> none  [the longest x1 7.05 us: body(): jnp.einsum('rcxy,rdxz->ycdz', p_routed, grouped_high, preferred_element_t...]
    all_to_all x0 -> x1, blocking collectives: none -> 24.8 us  [body(): mine = lax.all_to_all(pair, 'z', 0, 0, tiled=True)]
    all_gather x0 -> x1, blocking collectives: none -> 18.7 us  [body(): whole = lax.all_gather(mine, ('z', 'core'), tiled=True)]
    reshape x1 -> x0, local copies, waits for them, and re-layouts: 12.7 us -> none  [body(): applied = applied.reshape(row_count, a_slots * p_slots, width, width)]
    pallas_call x0 -> x2, Pallas kernels: none -> 5.44 us  [the longest x1 3.83 us: body(): pl.pallas_call(functools.partial(own_kernel, fr, ka, b), out_shape=[jax.S...]
    unnamed x5 -> x8, local copies, waits for them, and re-layouts: 0.11 us -> 5.28 us
    dynamic_update_slice x4 -> x0, local copies, waits for them, and re-layouts: 4.75 us -> none  [body(): lax.map(product_group, (a_local.reshape(group_count, group_rows, a_slots,...]
  transfers between devices with their start and end apart: 3 -> 3, of which waited for: 1 -> 2; matrix products, arithmetic and copies ran while one was open for 4% -> 1% of each run, Pallas kernels for 0% -> 6%
where the time goes in v1:
time: 69.1 us; the launch traced here: 68.7 us
  blocking collectives  43.5 us (63%)
  starting transfers between devices  11.1 us (16%)
  local copies, waits for them, and re-layouts  6.34 us (9%)
  Pallas kernels  5.44 us (8%)
  waiting for transfers between devices  2.11 us (3%)
    all_to_all x1, blocking collectives, body(): mine = lax.all_to_all(pair, 'z', 0, 0, tiled=True)  24.8 us
    all_gather x1, blocking collectives, body(): whole = lax.all_gather(mine, ('z', 'core'), tiled=True)  18.7 us
    ppermute x1, starting transfers between devices, body(): hi = lax.ppermute(p_local[:HB], 'agg', backward)  5.36 us
    unnamed x8, local copies, waits for them, and re-layouts  5.28 us
    pallas_call x1, Pallas kernels, body(): pl.pallas_call(functools.partial(own_kernel, fr, ka, b), out_shape=[jax.S...  3.83 us
    ppermute x1, starting transfers between devices, body(): got = lax.ppermute(send, 'core', [(0, 1), (1, 0)])  3.77 us
    ppermute x1, starting transfers between devices, body(): lo = lax.ppermute(p_local[fr - HB:], 'agg', forward)  1.92 us
    pallas_call x1, Pallas kernels, body(): pl.pallas_call(functools.partial(halo_kernel, fr, ka, b, pieces, regions)...  1.61 us
  transfers between devices with their start and end apart: 3, of which 2 were waited for; matrix products, arithmetic and copies ran while one was open for 1% of the time, Pallas kernels for 6%

profile of v1, /device:TPU:7, one launch (start us, length us, event | category | flops | bytes accessed | tf_op | source)
XLA Modules:
  0.0 68.7 jit_solution(1487595887774752425)
XLA Ops:
  0.0 1.1 %slice_bitcast_fusion = (bf16[4,2,128,128]{3,2,1,0:T(8,128)(2,1)S(1)}, bf16[4,2,128,128]{3,2,1,0:T(8,128)(2,1)S(1)}) fusion(bf16[1,1,16,2,128,128]{5,4,3,2,1,0:T(8,128)(2,1)} %param.6), kind=kLoop, calls=%fused_computation.1 | loop fusion | bytes 1048576 | tf_op jit(solution)/shard_map/slice | solution.py:118
  1.1 5.4 %collective-permute-start.1 = (bf16[4,2,128,128]{3,2,1,0:T(8,128)(2,1)S(1)}, bf16[4,2,128,128]{3,2,1,0:T(8,128)(2,1)S(1)}, u32[]{:S(2)}, u32[]{:S(2)}) collective-permute-start(bf16[4,2,128,128]{3,2,1,0:T(8,128)(2,1)S(1)} %get-tuple-element.15), channel_id=1, source_target_pairs={{16,0},{32,16},{48,32},{64,48},{80,64},{96,80},{112,96},{128,112},... | collective-permute-start | bytes 786440 | tf_op jit(solution)/shard_map/ppermute | solution.py:118
  6.4 1.9 %collective-permute-start = (bf16[4,2,128,128]{3,2,1,0:T(8,128)(2,1)S(1)}, bf16[4,2,128,128]{3,2,1,0:T(8,128)(2,1)S(1)}, u32[]{:S(2)}, u32[]{:S(2)}) collective-permute-start(bf16[4,2,128,128]{3,2,1,0:T(8,128)(2,1)S(1)} %get-tuple-element.16), channel_id=1, source_target_pairs={{0,16},{16,32},{32,48},{48,64},{64,80},{80,96},{96,112},{112,128},... | collective-permute-start | bytes 786440 | tf_op jit(solution)/shard_map/ppermute | solution.py:117
  8.4 0.7 %copy.7 = s32[1,1,16,5]{2,3,1,0:T(8,128)S(1)} copy(s32[1,1,16,5]{2,1,3,0:T(1,128)} %param.5) | data formatting | bytes 640
  9.1 0.0 copy-start
  9.1 1.2 %copy-done = bf16[1,1,16,2,128,128]{5,4,3,2,1,0:T(8,128)(2,1)S(1)} copy-done((bf16[1,1,16,2,128,128]{5,4,3,2,1,0:T(8,128)(2,1)S(1)}, bf16[1,1,16,2,128,128]{5,4,3,2,1,0:T(8,128)(2,1)}, u32[]{:S(2)}) %copy-start) | copy-done | bytes 1048600
  10.3 0.0 copy-start.1
  10.3 0.7 %copy-done.1 = s32[32,1,16,2]{0,3,2,1:T(2,128)S(1)} copy-done((s32[32,1,16,2]{0,3,2,1:T(2,128)S(1)}, s32[32,1,16,2]{0,3,2,1:T(2,128)}, u32[]{:S(2)}) %copy-start.1) | copy-done | bytes 4120
  11.0 0.0 copy-start.2
  11.0 1.7 %copy-done.2 = bf16[1,1,16,5,128,128]{5,4,3,2,1,0:T(8,128)(2,1)S(1)} copy-done((bf16[1,1,16,5,128,128]{5,4,3,2,1,0:T(8,128)(2,1)S(1)}, bf16[1,1,16,5,128,128]{5,4,3,2,1,0:T(8,128)(2,1)}, u32[]{:S(2)}) %copy-start.2) | copy-done | bytes 2621464
  12.7 3.8 %own_part.1 = (bf16[384,384]{1,0:T(8,128)(2,1)S(1)}, bf16[384,512]{1,0:T(8,128)(2,1)S(1)}, bf16[384,512]{1,0:T(8,128)(2,1)S(1)}) custom-call(s32[5,16]{1,0:T(8,128)S(1)} %bitcast.24, s32[32,32]{1,0:T(8,128)S(1)} %bitcast.22, bf16[16,5,128,128]{3,2,1,0:T(8,128)(2,1)S(1)} %bitcast.26, bf16[16,2,128,128]{3,2,1,0:T(8,128)(2,1)S(1)} %bitcast.21), custom_call_target="tpu_custom_call" | custom-call | flops 2000000000 | bytes 6000000 | tf_op jit(solution)/shard_map/own_part/pallas_call | solution.py:123
  16.6 0.0 collective-permute-done.1.hi
  16.6 0.7 %collective-permute-done.lo = bf16[4,2,128,128]{3,2,1,0:T(8,128)(2,1)S(1)} collective-permute-done((bf16[4,2,128,128]{3,2,1,0:T(8,128)(2,1)S(1)}, bf16[4,2,128,128]{3,2,1,0:T(8,128)(2,1)S(1)}, u32[]{:S(2)}, u32[]{:S(2)}) %collective-permute-start) | collective-permute-done | bytes 262176 | tf_op jit(solution)/shard_map/ppermute | solution.py:117
  17.3 1.6 %halo_part.1 = (bf16[8,216,128]{2,1,0:T(8,128)(2,1)S(1)}, bf16[8,216,128]{2,1,0:T(8,128)(2,1)S(1)}) custom-call(s32[5,16]{1,0:T(8,128)S(1)} %bitcast.25, s32[32,32]{1,0:T(8,128)S(1)} %bitcast.23, bf16[384,384]{1,0:T(8,128)(2,1)S(1)} %get-tuple-element.10.own, bf16[384,512]{1,0:T(8,128)(2,1)S(1)} %get-tuple-element.11.w_lo, ...), custom_call_target="tpu_custom_call" | custom-call | flops 400000000 | bytes 3000000 | tf_op jit(solution)/shard_map/halo_part/pallas_call | solution.py:141
  18.9 3.8 %collective-permute-start.2 = (bf16[8,216,128]{2,1,0:T(8,128)(2,1)S(1)}, bf16[8,216,128]{2,1,0:T(8,128)(2,1)S(1)}, u32[]{:S(2)}, u32[]{:S(2)}) collective-permute-start(bf16[8,216,128]{2,1,0:T(8,128)(2,1)S(1)} %get-tuple-element.14), channel_id=1, source_target_pairs={{0,1},{1,0},{2,3},{3,2},{4,5},{5,4},{6,7},{7,6},{8,9},{9,8},{10,11... | collective-permute-start | bytes 1327112 | tf_op jit(solution)/shard_map/ppermute | solution.py:152
  22.7 1.4 %collective-permute-done.2 = bf16[8,216,128]{2,1,0:T(8,128)(2,1)S(1)} collective-permute-done((bf16[8,216,128]{2,1,0:T(8,128)(2,1)S(1)}, bf16[8,216,128]{2,1,0:T(8,128)(2,1)S(1)}, u32[]{:S(2)}, u32[]{:S(2)}) %collective-permute-start.2) | collective-permute-done | bytes 442400 | tf_op jit(solution)/shard_map/ppermute | solution.py:152
  24.1 0.1 add_convert_fusion
  24.2 24.8 %all_to_all.5 = bf16[8,216,128]{2,1,0:T(8,128)(2,1)S(1)} all-to-all(bf16[8,216,128]{2,1,0:T(8,128)(2,1)S(1)} %add_convert_fusion), channel_id=1, replica_groups=mesh['agg'=32,'z'=8,'core'=2] {'z'}, dimensions={0} | all-to-all | bytes 884736 | tf_op jit(solution)/shard_map/all_to_all | solution.py:154
  49.0 0.1 reduce_sum.12
  49.0 18.7 %all_gather.3 = bf16[3456,128]{1,0:T(8,128)(2,1)S(1)} all-gather(bf16[216,128]{1,0:T(8,128)(2,1)S(1)} %reduce_sum.12), channel_id=1, replica_groups=mesh['agg'=32,'z'=8,'core'=2] {'z','core'}, dimensions={0}, use_global_device_ids=true | all-gather | bytes 940032 | tf_op jit(solution)/shard_map/all_gather | solution.py:156
  67.8 0.9 %copy.9 = bf16[1,128,3,9,128]{4,1,3,2,0:T(8,128)(2,1)} copy(bf16[1,128,3,9,128]{4,1,3,2,0:T(8,128)(2,1)S(1)} %bitcast.27) | data formatting | bytes 1769472
Async XLA Ops:
  1.1 15.5 %collective-permute-start.1 = (bf16[4,2,128,128]{3,2,1,0:T(8,128)(2,1)S(1)}, bf16[4,2,128,128]{3,2,1,0:T(8,128)(2,1)S(1)}, u32[]{:S(2)}, u32[]{:S(2)}) collective-permute-start(bf16[4,2,128,128]{3,2,1,0:T(8,128)(2,1)S(1)} %get-tuple-element.15), channel_id=1, source_target_pairs={{16,0},{32,16},{48,32},{64,48},{80,64},{96,80},{112,96},{128,112},... | collective-permute-start | bytes 786440 | tf_op jit(solution)/shard_map/ppermute | solution.py:118
  6.4 10.9 %collective-permute-start = (bf16[4,2,128,128]{3,2,1,0:T(8,128)(2,1)S(1)}, bf16[4,2,128,128]{3,2,1,0:T(8,128)(2,1)S(1)}, u32[]{:S(2)}, u32[]{:S(2)}) collective-permute-start(bf16[4,2,128,128]{3,2,1,0:T(8,128)(2,1)S(1)} %get-tuple-element.16), channel_id=1, source_target_pairs={{0,16},{16,32},{32,48},{48,64},{64,80},{80,96},{96,112},{112,128},... | collective-permute-start | bytes 786440 | tf_op jit(solution)/shard_map/ppermute | solution.py:117
  9.1 1.2 %copy-start = (bf16[1,1,16,2,128,128]{5,4,3,2,1,0:T(8,128)(2,1)S(1)}, bf16[1,1,16,2,128,128]{5,4,3,2,1,0:T(8,128)(2,1)}, u32[]{:S(2)}) copy-start(bf16[1,1,16,2,128,128]{5,4,3,2,1,0:T(8,128)(2,1)} %param.6) | copy-start | bytes 3145732
  10.3 0.7 %copy-start.1 = (s32[32,1,16,2]{0,3,2,1:T(2,128)S(1)}, s32[32,1,16,2]{0,3,2,1:T(2,128)}, u32[]{:S(2)}) copy-start(s32[32,1,16,2]{0,3,2,1:T(2,128)} %param.7) | copy-start | bytes 12292
  11.0 1.7 %copy-start.2 = (bf16[1,1,16,5,128,128]{5,4,3,2,1,0:T(8,128)(2,1)S(1)}, bf16[1,1,16,5,128,128]{5,4,3,2,1,0:T(8,128)(2,1)}, u32[]{:S(2)}) copy-start(bf16[1,1,16,5,128,128]{5,4,3,2,1,0:T(8,128)(2,1)} %param.4) | copy-start | bytes 7864324
  18.9 5.2 %collective-permute-start.2 = (bf16[8,216,128]{2,1,0:T(8,128)(2,1)S(1)}, bf16[8,216,128]{2,1,0:T(8,128)(2,1)S(1)}, u32[]{:S(2)}, u32[]{:S(2)}) collective-permute-start(bf16[8,216,128]{2,1,0:T(8,128)(2,1)S(1)} %get-tuple-element.14), channel_id=1, source_target_pairs={{0,1},{1,0},{2,3},{3,2},{4,5},{5,4},{6,7},{7,6},{8,9},{9,8},{10,11... | collective-permute-start | bytes 1327112 | tf_op jit(solution)/shard_map/ppermute | solution.py:152

commit v2 on v1

v2 whole, which is shorter than its diff:
```python
import functools

import jax
import jax.numpy as jnp
from jax import lax
from jax.experimental import pallas as pl
from jax.experimental.pallas import tpu as pltpu
from jax.sharding import Mesh
from jax.sharding import PartitionSpec as P

NC = 3
HB = 4
F32 = jnp.float32
BF16 = jnp.bfloat16


def contract_rows(a, b):
    return lax.dot_general(a, b, (((0,), (0,)), ((), ())), preferred_element_type=F32)


def own_kernel(fr, ka, b, chunks, acol_hbm, pcol_hbm, a_hbm, p_hbm, own, v_lo, v_hi, mask, acol, pcol, a, p, routed, grouped, summed, sems):
    region = lax.axis_index("agg")
    last = lax.axis_size("agg") - 1
    step = fr // chunks
    copies = [
        pltpu.make_async_copy(pcol_hbm, pcol, sems.at[0]),
        pltpu.make_async_copy(p_hbm, p, sems.at[1]),
        pltpu.make_async_copy(acol_hbm, acol, sems.at[2]),
    ]
    for i in range(chunks):
        rows = pl.ds(i * step, step)
        copies.append(pltpu.make_async_copy(a_hbm.at[rows], a.at[rows], sems.at[3 + i]))
    for copy in copies:
        copy.start()

    zeros = jnp.zeros((b, b), BF16)
    for d in range(NC):
        routed[d, pl.ds(fr * b, b), :] = zeros
    copies[0].wait()
    mask[...] = jnp.zeros_like(mask)
    one = jnp.ones(mask.shape[-2:], BF16)
    for side, source, first_row in ((0, jnp.maximum(region - 1, 0), fr - HB), (1, jnp.minimum(region + 1, last), 0)):
        for j in range(HB):
            for m in range(2):
                mask[side, j, m, pcol[first_row + j, m, source]] = one
    copies[1].wait()
    for r in range(fr):
        first, second = pcol[r, 0, region], pcol[r, 1, region]
        rows = pl.ds(r * b, b)
        routed[first, rows, :] = p[r, 0]
        routed[second, rows, :] = p[r, 1]
        routed[NC - first - second, rows, :] = zeros
    copies[2].wait()

    def block_row(start):
        rows = pl.ds(pl.multiple_of(start, b), b)
        return jnp.concatenate([routed[d, rows, :] for d in range(NC)], axis=1)

    for r in range(fr):
        if r % step == 0:
            copies[3 + r // step].wait()
        starts = []
        for k in range(ka):
            col = acol[k, 0, r]
            own_row = (col >= HB) & (col < HB + fr)
            starts.append(jnp.where(own_row, col - HB, fr) * b)
        left = jnp.concatenate([a[r, k] for k in range(ka)], axis=1)
        right = jnp.concatenate([block_row(s) for s in starts], axis=0)
        g = jnp.dot(left, right, preferred_element_type=F32)
        grouped[pl.ds(r * b, b), :] = g.astype(BF16)
    every = jnp.concatenate([routed[d, pl.ds(0, fr * b), :] for d in range(NC)], axis=1)
    own[...] = contract_rows(every, grouped[...]).astype(BF16)

    for out, first_row, slot, base in ((v_lo, 0, 1, 0), (v_hi, fr - HB, ka - 1, HB + fr)):
        summed[...] = jnp.zeros_like(summed)
        for i in range(HB):
            r = first_row + i
            j = acol[slot, 0, r] - base

            @pl.when((j >= 0) & (j < HB))
            def _(r=r, j=j, slot=slot):
                summed[jnp.clip(j, 0, HB - 1)] += contract_rows(block_row(r * b), a[r, slot])

        for j in range(HB):
            out[:, pl.ds(j * b, b)] = summed[j].astype(BF16)


def halo_kernel(b, pieces, own, v_lo, v_hi, mask, lo, hi, keep, send):
    core = lax.axis_index("core")
    band = 3 * NC
    per = NC * band * b // pieces
    tile = mask.shape[-2]

    def halo_part(side, v, halo):
        columns = []
        for d in range(NC):
            rows = []
            for j in range(HB):
                terms = [halo[j, m].reshape(b // tile, tile, b) * mask[side, j, m, d][None] for m in range(2)]
                rows.append((terms[0] + terms[1]).reshape(b, b))
            columns.append(jnp.concatenate(rows, axis=0))
        right = jnp.concatenate(columns, axis=1)
        return jnp.dot(v[...], right, preferred_element_type=F32).astype(BF16)

    parts = [halo_part(0, v_lo, lo), own[...], halo_part(1, v_hi, hi)]

    def write(even, odd):
        for c in range(NC):
            for d in range(band):
                block = parts[d // NC][c * b : (c + 1) * b, (d % NC) * b : (d % NC + 1) * b]
                at = (c * band + d) * b
                done = 0
                while done < b:
                    q, offset = divmod(at + done, per)
                    count = min(b - done, per - offset)
                    (even, odd)[q % 2][q // 2, offset : offset + count, :] = block[done : done + count]
                    done += count

    @pl.when(core == 0)
    def _():
        write(keep, send)

    @pl.when(core == 1)
    def _():
        write(send, keep)


def body(a_blocks, a_cols, p_blocks, p_cols):
    a_local, p_local = a_blocks[0, 0], p_blocks[0, 0]
    fr, ka, b = a_local.shape[:3]
    regions = p_cols.shape[0]
    acol = a_cols[0].transpose(2, 0, 1)
    pcol = p_cols[:, 0].transpose(1, 2, 0)
    band = 3 * NC
    chunks = 4
    z_count, core_count = lax.axis_size("z"), lax.axis_size("core")
    pieces = z_count * core_count
    per = NC * band * b // pieces
    forward = [(i, i + 1) for i in range(regions - 1)]
    backward = [(target, source) for source, target in forward]
    lo = lax.ppermute(p_local[fr - HB :], "agg", forward)
    hi = lax.ppermute(p_local[:HB], "agg", backward)

    vmem = pl.BlockSpec(memory_space=pltpu.VMEM)
    hbm = pl.BlockSpec(memory_space=pltpu.HBM)
    n = NC * b
    own, v_lo, v_hi, mask = pl.pallas_call(
        functools.partial(own_kernel, fr, ka, b, chunks),
        out_shape=[
            jax.ShapeDtypeStruct((n, n), BF16),
            jax.ShapeDtypeStruct((n, HB * b), BF16),
            jax.ShapeDtypeStruct((n, HB * b), BF16),
            jax.ShapeDtypeStruct((2, HB, 2, NC, 16, b), BF16),
        ],
        in_specs=[hbm] * 4,
        out_specs=[vmem] * 4,
        scratch_shapes=[
            pltpu.SMEM(acol.shape, jnp.int32),
            pltpu.SMEM(pcol.shape, jnp.int32),
            pltpu.VMEM(a_local.shape, BF16),
            pltpu.VMEM(p_local.shape, BF16),
            pltpu.VMEM((NC, (fr + 1) * b, b), BF16),
            pltpu.VMEM((fr * b, n), BF16),
            pltpu.VMEM((HB, n, b), F32),
            pltpu.SemaphoreType.DMA((3 + chunks,)),
        ],
        cost_estimate=pl.CostEstimate(flops=2_000_000_000, bytes_accessed=6_000_000, transcendentals=0),
        compiler_params=pltpu.CompilerParams(vmem_limit_bytes=40 << 20),
        name="own_part",
    )(*[pltpu.with_memory_space_constraint(x, pltpu.HBM) for x in (acol, pcol, a_local, p_local)])

    keep, send = pl.pallas_call(
        functools.partial(halo_kernel, b, pieces),
        out_shape=[jax.ShapeDtypeStruct((z_count, per, b), BF16)] * 2,
        in_specs=[vmem] * 6,
        out_specs=[vmem] * 2,
        cost_estimate=pl.CostEstimate(flops=400_000_000, bytes_accessed=3_000_000, transcendentals=0),
        compiler_params=pltpu.CompilerParams(vmem_limit_bytes=20 << 20),
        name="halo_part",
    )(own, v_lo, v_hi, mask, lo, hi)

    sent = lax.all_gather(send, "core")
    got = lax.dynamic_index_in_dim(sent, 1 - lax.axis_index("core"), 0, keepdims=False)
    pair = (keep.astype(F32) + got.astype(F32)).astype(BF16)
    mine = lax.all_to_all(pair, "z", 0, 0, tiled=True)
    mine = mine.astype(F32).sum(0).astype(BF16)
    whole = lax.all_gather(mine, ("z", "core"), tiled=True)
    return whole.reshape(NC, band, b, b).transpose(2, 0, 1, 3)[None]


def solution(mesh):
    agg, grp = mesh.devices.shape
    split = Mesh(mesh.devices.reshape(agg, grp // 2, 2), ("agg", "z", "core"))
    both = ("z", "core")
    return jax.shard_map(
        body,
        mesh=split,
        in_specs=(
            P("agg", both, None, None, None, None),
            P("agg", both, None, None),
            P("agg", both, None, None, None, None),
            P(None, both, None, None),
        ),
        out_specs=P("agg", None, None, None, None),
        check_vma=False,
    )
```

time: 69.1 us -> 64.9 us (0.939)
  the two profiles are of different devices: /device:TPU:7 before, /device:TPU:29 now
where the time goes in v2:
time: 64.9 us; the launch traced here: 64.7 us
  blocking collectives  47.4 us (73%)
  Pallas kernels  7.05 us (11%)
  starting transfers between devices  6.34 us (10%)
  local copies, waits for them, and re-layouts  1.98 us (3%)
  waiting for transfers between devices  1.65 us (3%)
    all_to_all x1, blocking collectives, body(): mine = lax.all_to_all(pair, 'z', 0, 0, tiled=True)  24.8 us
    all_gather x1, blocking collectives, body(): whole = lax.all_gather(mine, ('z', 'core'), tiled=True)  18.7 us
    pallas_call x1, Pallas kernels, body(): pl.pallas_call(functools.partial(own_kernel, fr, ka, b, chunks), out_shap...  6.36 us
    ppermute x1, starting transfers between devices, body(): lo = lax.ppermute(p_local[fr - HB:], 'agg', forward)  4.42 us
    all_gather x1, blocking collectives, body(): sent = lax.all_gather(send, 'core')  3.9 us
    ppermute x1, starting transfers between devices, body(): hi = lax.ppermute(p_local[:HB], 'agg', backward)  1.92 us
    ppermute x1, waiting for transfers between devices, body(): hi = lax.ppermute(p_local[:HB], 'agg', backward)  1.65 us
  transfers between devices with their start and end apart: 2, of which 1 were waited for; matrix products, arithmetic and copies ran while one was open for 0% of the time, Pallas kernels for 10%

profile of v2, /device:TPU:29, one launch (start us, length us, event | category | flops | bytes accessed | tf_op | source)
XLA Modules:
  0.0 64.7 jit_solution(12801592693960837024)
XLA Ops:
  0.0 1.1 %slice_bitcast_fusion = (bf16[4,2,128,128]{3,2,1,0:T(8,128)(2,1)S(1)}, bf16[4,2,128,128]{3,2,1,0:T(8,128)(2,1)S(1)}) fusion(bf16[1,1,16,2,128,128]{5,4,3,2,1,0:T(8,128)(2,1)} %param.6), kind=kLoop, calls=%fused_computation.2 | loop fusion | bytes 1048576 | tf_op jit(solution)/shard_map/slice | solution.py:142
  1.1 4.4 %collective-permute-start = (bf16[4,2,128,128]{3,2,1,0:T(8,128)(2,1)S(1)}, bf16[4,2,128,128]{3,2,1,0:T(8,128)(2,1)S(1)}, u32[]{:S(2)}, u32[]{:S(2)}) collective-permute-start(bf16[4,2,128,128]{3,2,1,0:T(8,128)(2,1)S(1)} %get-tuple-element.18), channel_id=1, source_target_pairs={{0,16},{16,32},{32,48},{48,64},{64,80},{80,96},{96,112},{112,128},... | collective-permute-start | bytes 786440 | tf_op jit(solution)/shard_map/ppermute | solution.py:141
  5.5 1.9 %collective-permute-start.1 = (bf16[4,2,128,128]{3,2,1,0:T(8,128)(2,1)S(1)}, bf16[4,2,128,128]{3,2,1,0:T(8,128)(2,1)S(1)}, u32[]{:S(2)}, u32[]{:S(2)}) collective-permute-start(bf16[4,2,128,128]{3,2,1,0:T(8,128)(2,1)S(1)} %get-tuple-element.17), channel_id=1, source_target_pairs={{16,0},{32,16},{48,32},{64,48},{80,64},{96,80},{112,96},{128,112},... | collective-permute-start | bytes 786440 | tf_op jit(solution)/shard_map/ppermute | solution.py:142
  7.4 6.4 %own_part.1 = (bf16[384,384]{1,0:T(8,128)(2,1)S(1)}, bf16[384,512]{1,0:T(8,128)(2,1)S(1)}, bf16[384,512]{1,0:T(8,128)(2,1)S(1)}, bf16[2,4,2,3,16,128]{5,4,3,2,1,0:T(8,128)(2,1)S(1)}) custom-call(s32[5,1,16]{2,1,0:T(1,128)} %bitcast.26, s32[16,2,32]{2,1,0:T(2,128)} %bitcast.25, bf16[16,5,128,128]{3,2,1,0:T(8,128)(2,1)} %bitcast.24, ...), custom_call_target="tpu_custom_call" | custom-call | flops 2000000000 | bytes 6000000 | tf_op jit(solution)/shard_map/own_part/pallas_call | solution.py:147
  13.8 0.0 collective-permute-done.lo
  13.8 1.6 %collective-permute-done.1.hi = bf16[4,2,128,128]{3,2,1,0:T(8,128)(2,1)S(1)} collective-permute-done((bf16[4,2,128,128]{3,2,1,0:T(8,128)(2,1)S(1)}, bf16[4,2,128,128]{3,2,1,0:T(8,128)(2,1)S(1)}, u32[]{:S(2)}, u32[]{:S(2)}) %collective-permute-start.1) | collective-permute-done | bytes 262176 | tf_op jit(solution)/shard_map/ppermute | solution.py:142
  15.5 0.7 %halo_part.1 = (bf16[8,216,128]{2,1,0:T(8,128)(2,1)S(1)}, bf16[8,216,128]{2,1,0:T(8,128)(2,1)S(1)}) custom-call(bf16[384,384]{1,0:T(8,128)(2,1)S(1)} %get-tuple-element.11.own, bf16[384,512]{1,0:T(8,128)(2,1)S(1)} %get-tuple-element.12.v_lo, bf16[384,512]{1,0:T(8,128)(2,1)S(1)} %get-tuple-element.13.v_hi, ...), custom_call_target="tpu_custom_call" | custom-call | flops 400000000 | bytes 3000000 | tf_op jit(solution)/shard_map/halo_part/pallas_call | solution.py:172
  16.2 3.9 %all-gather = bf16[16,216,128]{2,1,0:T(8,128)(2,1)S(1)} all-gather(bf16[8,216,128]{2,1,0:T(8,128)(2,1)S(1)} %get-tuple-element.16), channel_id=2, replica_groups=mesh['agg'=32,'z'=8,'core'=2] {'core'}, dimensions={0}, use_global_device_ids=true | all-gather | bytes 1327104 | tf_op jit(solution)/shard_map/all_gather | solution.py:182
  20.1 0.1 fusion
  20.2 24.8 %all_to_all.5 = bf16[8,216,128]{2,1,0:T(8,128)(2,1)S(1)} all-to-all(bf16[8,216,128]{2,1,0:T(8,128)(2,1)S(1)} %fusion), channel_id=1, replica_groups=mesh['agg'=32,'z'=8,'core'=2] {'z'}, dimensions={0} | all-to-all | bytes 884736 | tf_op jit(solution)/shard_map/all_to_all | solution.py:185
  45.0 0.1 reduce_sum.12
  45.0 18.7 %all_gather.11 = bf16[3456,128]{1,0:T(8,128)(2,1)S(1)} all-gather(bf16[216,128]{1,0:T(8,128)(2,1)S(1)} %reduce_sum.12), channel_id=1, replica_groups=mesh['agg'=32,'z'=8,'core'=2] {'z','core'}, dimensions={0}, use_global_device_ids=true | all-gather | bytes 940032 | tf_op jit(solution)/shard_map/all_gather | solution.py:187
  63.7 0.9 %copy.6 = bf16[1,128,3,9,128]{4,1,3,2,0:T(8,128)(2,1)} copy(bf16[1,128,3,9,128]{4,1,3,2,0:T(8,128)(2,1)S(1)} %bitcast.21) | data formatting | bytes 1769472
Async XLA Ops:
  1.1 12.7 %collective-permute-start = (bf16[4,2,128,128]{3,2,1,0:T(8,128)(2,1)S(1)}, bf16[4,2,128,128]{3,2,1,0:T(8,128)(2,1)S(1)}, u32[]{:S(2)}, u32[]{:S(2)}) collective-permute-start(bf16[4,2,128,128]{3,2,1,0:T(8,128)(2,1)S(1)} %get-tuple-element.18), channel_id=1, source_target_pairs={{0,16},{16,32},{32,48},{48,64},{64,80},{80,96},{96,112},{112,128},... | collective-permute-start | bytes 786440 | tf_op jit(solution)/shard_map/ppermute | solution.py:141
  5.5 10.0 %collective-permute-start.1 = (bf16[4,2,128,128]{3,2,1,0:T(8,128)(2,1)S(1)}, bf16[4,2,128,128]{3,2,1,0:T(8,128)(2,1)S(1)}, u32[]{:S(2)}, u32[]{:S(2)}) collective-permute-start(bf16[4,2,128,128]{3,2,1,0:T(8,128)(2,1)S(1)} %get-tuple-element.17), channel_id=1, source_target_pairs={{16,0},{32,16},{48,32},{64,48},{80,64},{96,80},{112,96},{128,112},... | collective-permute-start | bytes 786440 | tf_op jit(solution)/shard_map/ppermute | solution.py:142

commit v3 on v2

--- a/solution.py
+++ b/solution.py
@@ -5,7 +5,6 @@
 from jax import lax
 from jax.experimental import pallas as pl
 from jax.experimental.pallas import tpu as pltpu
-from jax.sharding import Mesh
 from jax.sharding import PartitionSpec as P
 
 NC = 3
@@ -18,7 +17,7 @@
     return lax.dot_general(a, b, (((0,), (0,)), ((), ())), preferred_element_type=F32)
 
 
-def own_kernel(fr, ka, b, chunks, acol_hbm, pcol_hbm, a_hbm, p_hbm, own, v_lo, v_hi, mask, acol, pcol, a, p, routed, grouped, summed, sems):
+def own_kernel(fr, ka, b, chunks, acol_hbm, pcol_hbm, a_hbm, p_hbm, own, v_first, v_second, mask, acol, pcol, a, p, routed, grouped, summed, sems):
     region = lax.axis_index("agg")
     last = lax.axis_size("agg") - 1
     step = fr // chunks
@@ -39,7 +38,11 @@
     copies[0].wait()
     mask[...] = jnp.zeros_like(mask)
     one = jnp.ones(mask.shape[-2:], BF16)
-    for side, source, first_row in ((0, jnp.maximum(region - 1, 0), fr - HB), (1, jnp.minimum(region + 1, last), 0)):
+    odd = lax.rem(region, 2)
+    for side in range(2):
+        low = odd == 1 - side
+        source = jnp.where(low, jnp.maximum(region - 1, 0), jnp.minimum(region + 1, last))
+        first_row = jnp.where(low, fr - HB, 0)
         for j in range(HB):
             for m in range(2):
                 mask[side, j, m, pcol[first_row + j, m, source]] = one
@@ -71,7 +74,9 @@
     every = jnp.concatenate([routed[d, pl.ds(0, fr * b), :] for d in range(NC)], axis=1)
     own[...] = contract_rows(every, grouped[...]).astype(BF16)
 
-    for out, first_row, slot, base in ((v_lo, 0, 1, 0), (v_hi, fr - HB, ka - 1, HB + fr)):
+    for side, out in enumerate((v_first, v_second)):
+        low = odd == 1 - side
+        first_row, slot, base = jnp.where(low, 0, fr - HB), jnp.where(low, 1, ka - 1), jnp.where(low, 0, HB + fr)
         summed[...] = jnp.zeros_like(summed)
         for i in range(HB):
             r = first_row + i
@@ -85,8 +90,9 @@
             out[:, pl.ds(j * b, b)] = summed[j].astype(BF16)
 
 
-def halo_kernel(b, pieces, own, v_lo, v_hi, mask, lo, hi, keep, send):
-    core = lax.axis_index("core")
+def halo_kernel(b, pieces, own, v_first, v_second, mask, first, second, keep, send):
+    core = lax.rem(lax.axis_index("grp"), 2)
+    odd = lax.rem(lax.axis_index("agg"), 2) == 1
     band = 3 * NC
     per = NC * band * b // pieces
     tile = mask.shape[-2]
@@ -102,9 +108,10 @@
         right = jnp.concatenate(columns, axis=1)
         return jnp.dot(v[...], right, preferred_element_type=F32).astype(BF16)
 
-    parts = [halo_part(0, v_lo, lo), own[...], halo_part(1, v_hi, hi)]
-
-    def write(even, odd):
+    by_first, by_second = halo_part(0, v_first, first), halo_part(1, v_second, second)
+    parts = [jnp.where(odd, by_first, by_second), own[...], jnp.where(odd, by_second, by_first)]
+
+    def write(even_core, odd_core):
         for c in range(NC):
             for d in range(band):
                 block = parts[d // NC][c * b : (c + 1) * b, (d % NC) * b : (d % NC + 1) * b]
@@ -113,7 +120,7 @@
                 while done < b:
                     q, offset = divmod(at + done, per)
                     count = min(b - done, per - offset)
-                    (even, odd)[q % 2][q // 2, offset : offset + count, :] = block[done : done + count]
+                    (even_core, odd_core)[q % 2][pieces // 2 - 1 - q // 2, offset : offset + count, :] = block[done : done + count]
                     done += count
 
     @pl.when(core == 0)
@@ -133,18 +140,22 @@
     pcol = p_cols[:, 0].transpose(1, 2, 0)
     band = 3 * NC
     chunks = 4
-    z_count, core_count = lax.axis_size("z"), lax.axis_size("core")
-    pieces = z_count * core_count
+    pieces = lax.axis_size("grp")
+    z_count = pieces // 2
     per = NC * band * b // pieces
-    forward = [(i, i + 1) for i in range(regions - 1)]
-    backward = [(target, source) for source, target in forward]
-    lo = lax.ppermute(p_local[fr - HB :], "agg", forward)
-    hi = lax.ppermute(p_local[:HB], "agg", backward)
+    odd = lax.rem(lax.axis_index("agg"), 2)
+
+    def swap(least, start):
+        pairs = [(i, i + 1) for i in range(least, regions - 1, 2)]
+        ends = lax.dynamic_slice_in_dim(p_local, start * (fr - HB), HB, 0)
+        return lax.ppermute(ends, "agg", pairs + [(j, i) for i, j in pairs])
+
+    first, second = swap(0, 1 - odd), swap(1, odd)
 
     vmem = pl.BlockSpec(memory_space=pltpu.VMEM)
     hbm = pl.BlockSpec(memory_space=pltpu.HBM)
     n = NC * b
-    own, v_lo, v_hi, mask = pl.pallas_call(
+    own, v_first, v_second, mask = pl.pallas_call(
         functools.partial(own_kernel, fr, ka, b, chunks),
         out_shape=[
             jax.ShapeDtypeStruct((n, n), BF16),
@@ -177,29 +188,30 @@
         cost_estimate=pl.CostEstimate(flops=400_000_000, bytes_accessed=3_000_000, transcendentals=0),
         compiler_params=pltpu.CompilerParams(vmem_limit_bytes=20 << 20),
         name="halo_part",
-    )(own, v_lo, v_hi, mask, lo, hi)
-
-    sent = lax.all_gather(send, "core")
-    got = lax.dynamic_index_in_dim(sent, 1 - lax.axis_index("core"), 0, keepdims=False)
+    )(own, v_first, v_second, mask, first, second)
+
+    chips = [[2 * z, 2 * z + 1] for z in range(z_count)]
+    same_core = [[2 * z + c for z in range(z_count)] for c in range(2)]
+    falling = [[2 * z + c for z in reversed(range(z_count)) for c in range(2)]]
+    sent = lax.all_gather(send, "grp", axis_index_groups=chips)
+    core = lax.rem(lax.axis_index("grp"), 2)
+    got = lax.dynamic_index_in_dim(sent, 1 - core, 0, keepdims=False)
     pair = (keep.astype(F32) + got.astype(F32)).astype(BF16)
-    mine = lax.all_to_all(pair, "z", 0, 0, tiled=True)
+    mine = lax.all_to_all(pair, "grp", 0, 0, tiled=True, axis_index_groups=same_core)
     mine = mine.astype(F32).sum(0).astype(BF16)
-    whole = lax.all_gather(mine, ("z", "core"), tiled=True)
+    whole = lax.all_gather(mine, "grp", tiled=True, axis_index_groups=falling)
     return whole.reshape(NC, band, b, b).transpose(2, 0, 1, 3)[None]
 
 
 def solution(mesh):
-    agg, grp = mesh.devices.shape
-    split = Mesh(mesh.devices.reshape(agg, grp // 2, 2), ("agg", "z", "core"))
-    both = ("z", "core")
     return jax.shard_map(
         body,
-        mesh=split,
+        mesh=mesh,
         in_specs=(
-            P("agg", both, None, None, None, None),
-            P("agg", both, None, None),
-            P("agg", both, None, None, None, None),
-            P(None, both, None, None),
+            P("agg", "grp", None, None, None, None),
+            P("agg", "grp", None, None),
+            P("agg", "grp", None, None, None, None),
+            P(None, "grp", None, None),
         ),
         out_specs=P("agg", None, None, None, None),
         check_vma=False,

time: 64.9 us -> 63.5 us (0.978)
  the two profiles are of different devices: /device:TPU:29 before, /device:TPU:7 now
where the time goes in v3:
time: 63.5 us; the launch traced here: 63.2 us
  blocking collectives  46.2 us (73%)
  starting transfers between devices  7.28 us (11%)
  Pallas kernels  7.1 us (11%)
  local copies, waits for them, and re-layouts  1.98 us (3%)
    all_to_all x1, blocking collectives, body(): lax.all_to_all(pair, 'grp', 0, 0, tiled=True, axis_index_groups=same_core)  24.8 us
    all_gather x1, blocking collectives, body(): whole = lax.all_gather(mine, 'grp', tiled=True, axis_index_groups=falling)  17.5 us
    ppermute x2, starting transfers between devices, swap(): return lax.ppermute(ends, 'agg', pairs + [(j, i) for i, j in pairs])  7.28 us
    pallas_call x1, Pallas kernels, body(): pl.pallas_call(functools.partial(own_kernel, fr, ka, b, chunks), out_shap...  6.4 us
    all_gather x1, blocking collectives, body(): sent = lax.all_gather(send, 'grp', axis_index_groups=chips)  3.93 us
  transfers between devices with their start and end apart: 2, of which 1 were waited for; matrix products, arithmetic and copies ran while one was open for 0% of the time, Pallas kernels for 10%

profile of v3, /device:TPU:7, one launch (start us, length us, event | category | flops | bytes accessed | tf_op | source)
XLA Modules:
  0.0 63.2 jit_solution(4015570215112176577)
XLA Ops:
  0.0 1.1 %dynamic-slice_bitcast_fusion = (bf16[4,2,128,128]{3,2,1,0:T(8,128)(2,1)S(1)}, bf16[4,2,128,128]{3,2,1,0:T(8,128)(2,1)S(1)}) fusion(bf16[1,1,16,2,128,128]{5,4,3,2,1,0:T(8,128)(2,1)} %param.6, s32[]{:T(128)S(6)} %select_n.11, s32[]{:T(128)S(6)} %select_n.10), kind=kLoop, calls=%fused_computation.2 | loop fusion | bytes 1048584 | tf_op jit(solution)/shard_map/dynamic_slice | solution.py:150
  1.1 5.4 %collective-permute-start.1 = (bf16[4,2,128,128]{3,2,1,0:T(8,128)(2,1)S(1)}, bf16[4,2,128,128]{3,2,1,0:T(8,128)(2,1)S(1)}, u32[]{:S(2)}, u32[]{:S(2)}) collective-permute-start(bf16[4,2,128,128]{3,2,1,0:T(8,128)(2,1)S(1)} %get-tuple-element.17), channel_id=1, source_target_pairs={{16,32},{48,64},{80,96},{112,128},{144,160},{176,192},{208,224},{2... | collective-permute-start | bytes 786440 | tf_op jit(solution)/shard_map/ppermute | solution.py:151
  6.4 1.9 %collective-permute-start = (bf16[4,2,128,128]{3,2,1,0:T(8,128)(2,1)S(1)}, bf16[4,2,128,128]{3,2,1,0:T(8,128)(2,1)S(1)}, u32[]{:S(2)}, u32[]{:S(2)}) collective-permute-start(bf16[4,2,128,128]{3,2,1,0:T(8,128)(2,1)S(1)} %get-tuple-element.18), channel_id=1, source_target_pairs={{0,16},{32,48},{64,80},{96,112},{128,144},{160,176},{192,208},{224... | collective-permute-start | bytes 786440 | tf_op jit(solution)/shard_map/ppermute | solution.py:151
  8.4 6.4 %own_part.1 = (bf16[384,384]{1,0:T(8,128)(2,1)S(1)}, bf16[384,512]{1,0:T(8,128)(2,1)S(1)}, bf16[384,512]{1,0:T(8,128)(2,1)S(1)}, bf16[2,4,2,3,16,128]{5,4,3,2,1,0:T(8,128)(2,1)S(1)}) custom-call(s32[5,1,16]{2,1,0:T(1,128)} %bitcast.26, s32[16,2,32]{2,1,0:T(2,128)} %bitcast.25, bf16[16,5,128,128]{3,2,1,0:T(8,128)(2,1)} %bitcast.24, ...), custom_call_target="tpu_custom_call" | custom-call | flops 2000000000 | bytes 6000000 | tf_op jit(solution)/shard_map/own_part/pallas_call | solution.py:158
  14.8 0.0 collective-permute-done.1.second
  14.8 0.4 collective-permute-done.first
  15.2 0.7 %halo_part.1 = (bf16[8,216,128]{2,1,0:T(8,128)(2,1)S(1)}, bf16[8,216,128]{2,1,0:T(8,128)(2,1)S(1)}) custom-call(bf16[384,384]{1,0:T(8,128)(2,1)S(1)} %get-tuple-element.11.own, bf16[384,512]{1,0:T(8,128)(2,1)S(1)} %get-tuple-element.12.v_first, bf16[384,512]{1,0:T(8,128)(2,1)S(1)} %get-tuple-element.13.v_second, ...), custom_call_target="tpu_custom_call" | custom-call | flops 400000000 | bytes 3000000 | tf_op jit(solution)/shard_map/halo_part/pallas_call | solution.py:183
  15.9 3.9 %all-gather = bf16[16,216,128]{2,1,0:T(8,128)(2,1)S(1)} all-gather(bf16[8,216,128]{2,1,0:T(8,128)(2,1)S(1)} %get-tuple-element.16), channel_id=2, replica_groups={{0,1},{2,3},{4,5},{6,7},{8,9},{10,11},{12,13},{14,15},{16,17},{18,19},{..., dimensions={0}, use_global_device_ids=true | all-gather | bytes 1327104 | tf_op jit(solution)/shard_map/all_gather | solution.py:196
  19.8 0.1 fusion
  19.9 24.8 %all_to_all.5 = bf16[8,216,128]{2,1,0:T(8,128)(2,1)S(1)} all-to-all(bf16[8,216,128]{2,1,0:T(8,128)(2,1)S(1)} %fusion), channel_id=1, replica_groups={{0,2,4,6,8,10,12,14},{1,3,5,7,9,11,13,15},{16,18,20,22,24,26,28,30},{17..., dimensions={0} | all-to-all | bytes 884736 | tf_op jit(solution)/shard_map/all_to_all | solution.py:200
  44.7 0.1 reduce_sum.12
  44.8 17.5 %all_gather.11 = bf16[3456,128]{1,0:T(8,128)(2,1)S(1)} all-gather(bf16[216,128]{1,0:T(8,128)(2,1)S(1)} %reduce_sum.12), channel_id=1, replica_groups={{14,15,12,13,10,11,8,9,6,7,4,5,2,3,0,1},{30,31,28,29,26,27,24,25,22,23,..., dimensions={0}, use_global_device_ids=true | all-gather | bytes 940032 | tf_op jit(solution)/shard_map/all_gather | solution.py:202
  62.3 0.9 %copy.6 = bf16[1,128,3,9,128]{4,1,3,2,0:T(8,128)(2,1)} copy(bf16[1,128,3,9,128]{4,1,3,2,0:T(8,128)(2,1)S(1)} %bitcast.21) | data formatting | bytes 1769472
Async XLA Ops:
  1.1 13.7 %collective-permute-start.1 = (bf16[4,2,128,128]{3,2,1,0:T(8,128)(2,1)S(1)}, bf16[4,2,128,128]{3,2,1,0:T(8,128)(2,1)S(1)}, u32[]{:S(2)}, u32[]{:S(2)}) collective-permute-start(bf16[4,2,128,128]{3,2,1,0:T(8,128)(2,1)S(1)} %get-tuple-element.17), channel_id=1, source_target_pairs={{16,32},{48,64},{80,96},{112,128},{144,160},{176,192},{208,224},{2... | collective-permute-start | bytes 786440 | tf_op jit(solution)/shard_map/ppermute | solution.py:151
  6.4 8.8 %collective-permute-start = (bf16[4,2,128,128]{3,2,1,0:T(8,128)(2,1)S(1)}, bf16[4,2,128,128]{3,2,1,0:T(8,128)(2,1)S(1)}, u32[]{:S(2)}, u32[]{:S(2)}) collective-permute-start(bf16[4,2,128,128]{3,2,1,0:T(8,128)(2,1)S(1)} %get-tuple-element.18), channel_id=1, source_target_pairs={{0,16},{32,48},{64,80},{96,112},{128,144},{160,176},{192,208},{224... | collective-permute-start | bytes 786440 | tf_op jit(solution)/shard_map/ppermute | solution.py:151

commit v4 on v3

--- a/solution.py
+++ b/solution.py
@@ -17,7 +17,7 @@
     return lax.dot_general(a, b, (((0,), (0,)), ((), ())), preferred_element_type=F32)
 
 
-def own_kernel(fr, ka, b, chunks, acol_hbm, pcol_hbm, a_hbm, p_hbm, own, v_first, v_second, mask, acol, pcol, a, p, routed, grouped, summed, sems):
+def own_kernel(fr, ka, b, chunks, acol_hbm, pcol_hbm, a_hbm, p_hbm, own, v_first, v_second, mask, acol, pcol, a, p, routed, grouped, sems):
     region = lax.axis_index("agg")
     last = lax.axis_size("agg") - 1
     step = fr // chunks
@@ -77,17 +77,15 @@
     for side, out in enumerate((v_first, v_second)):
         low = odd == 1 - side
         first_row, slot, base = jnp.where(low, 0, fr - HB), jnp.where(low, 1, ka - 1), jnp.where(low, 0, HB + fr)
-        summed[...] = jnp.zeros_like(summed)
+        rows = []
         for i in range(HB):
             r = first_row + i
+            block = a[r, slot]
             j = acol[slot, 0, r] - base
-
-            @pl.when((j >= 0) & (j < HB))
-            def _(r=r, j=j, slot=slot):
-                summed[jnp.clip(j, 0, HB - 1)] += contract_rows(block_row(r * b), a[r, slot])
-
-        for j in range(HB):
-            out[:, pl.ds(j * b, b)] = summed[j].astype(BF16)
+            rows.append(jnp.concatenate([jnp.where(j == t, block, zeros) for t in range(HB)], axis=1))
+        here = pl.ds(pl.multiple_of(first_row * b, b), HB * b)
+        left = jnp.concatenate([routed[d, here, :] for d in range(NC)], axis=1)
+        out[...] = contract_rows(left, jnp.concatenate(rows, axis=0)).astype(BF16)
 
 
 def halo_kernel(b, pieces, own, v_first, v_second, mask, first, second, keep, send):
@@ -120,7 +118,8 @@
                 while done < b:
                     q, offset = divmod(at + done, per)
                     count = min(b - done, per - offset)
-                    (even_core, odd_core)[q % 2][pieces // 2 - 1 - q // 2, offset : offset + count, :] = block[done : done + count]
+                    at_slot = pieces // 2 - 1 - q // 2 if q % 2 else q // 2
+                    (even_core, odd_core)[q % 2][at_slot, offset : offset + count, :] = block[done : done + count]
                     done += count
 
     @pl.when(core == 0)
@@ -132,30 +131,15 @@
         write(send, keep)
 
 
-def body(a_blocks, a_cols, p_blocks, p_cols):
-    a_local, p_local = a_blocks[0, 0], p_blocks[0, 0]
+def first_kernel(a_local, a_cols, p_local, p_cols):
     fr, ka, b = a_local.shape[:3]
-    regions = p_cols.shape[0]
     acol = a_cols[0].transpose(2, 0, 1)
     pcol = p_cols[:, 0].transpose(1, 2, 0)
-    band = 3 * NC
     chunks = 4
-    pieces = lax.axis_size("grp")
-    z_count = pieces // 2
-    per = NC * band * b // pieces
-    odd = lax.rem(lax.axis_index("agg"), 2)
-
-    def swap(least, start):
-        pairs = [(i, i + 1) for i in range(least, regions - 1, 2)]
-        ends = lax.dynamic_slice_in_dim(p_local, start * (fr - HB), HB, 0)
-        return lax.ppermute(ends, "agg", pairs + [(j, i) for i, j in pairs])
-
-    first, second = swap(0, 1 - odd), swap(1, odd)
-
     vmem = pl.BlockSpec(memory_space=pltpu.VMEM)
     hbm = pl.BlockSpec(memory_space=pltpu.HBM)
     n = NC * b
-    own, v_first, v_second, mask = pl.pallas_call(
+    return pl.pallas_call(
         functools.partial(own_kernel, fr, ka, b, chunks),
         out_shape=[
             jax.ShapeDtypeStruct((n, n), BF16),
@@ -172,13 +156,33 @@
             pltpu.VMEM(p_local.shape, BF16),
             pltpu.VMEM((NC, (fr + 1) * b, b), BF16),
             pltpu.VMEM((fr * b, n), BF16),
-            pltpu.VMEM((HB, n, b), F32),
             pltpu.SemaphoreType.DMA((3 + chunks,)),
         ],
         cost_estimate=pl.CostEstimate(flops=2_000_000_000, bytes_accessed=6_000_000, transcendentals=0),
         compiler_params=pltpu.CompilerParams(vmem_limit_bytes=40 << 20),
         name="own_part",
     )(*[pltpu.with_memory_space_constraint(x, pltpu.HBM) for x in (acol, pcol, a_local, p_local)])
+
+
+def body(a_blocks, a_cols, p_blocks, p_cols):
+    a_local, p_local = a_blocks[0, 0], p_blocks[0, 0]
+    fr, ka, b = a_local.shape[:3]
+    regions = p_cols.shape[0]
+    band = 3 * NC
+    pieces = lax.axis_size("grp")
+    z_count = pieces // 2
+    per = NC * band * b // pieces
+    odd = lax.rem(lax.axis_index("agg"), 2)
+
+    def swap(least, start):
+        pairs = [(i, i + 1) for i in range(least, regions - 1, 2)]
+        ends = lax.dynamic_slice_in_dim(p_local, start * (fr - HB), HB, 0)
+        return lax.ppermute(ends, "agg", pairs + [(j, i) for i, j in pairs])
+
+    first, second = swap(0, 1 - odd), swap(1, odd)
+
+    vmem = pl.BlockSpec(memory_space=pltpu.VMEM)
+    own, v_first, v_second, mask = first_kernel(a_local, a_cols, p_local, p_cols)
 
     keep, send = pl.pallas_call(
         functools.partial(halo_kernel, b, pieces),
@@ -191,7 +195,7 @@
     )(own, v_first, v_second, mask, first, second)
 
     chips = [[2 * z, 2 * z + 1] for z in range(z_count)]
-    same_core = [[2 * z + c for z in range(z_count)] for c in range(2)]
+    same_core = [[2 * z for z in reversed(range(z_count))], [2 * z + 1 for z in range(z_count)]]
     falling = [[2 * z + c for z in reversed(range(z_count)) for c in range(2)]]
     sent = lax.all_gather(send, "grp", axis_index_groups=chips)
     core = lax.rem(lax.axis_index("grp"), 2)

time: 63.5 us -> 62.7 us (0.987)
  waiting for transfers between devices: 0.4 us -> 1.87 us
  Pallas kernels: 7.1 us -> 5.63 us
  blocking collectives: 46.2 us -> 45.4 us
    ppermute x2, waiting for transfers between devices: 0.4 us -> 1.87 us  [swap(): return lax.ppermute(ends, 'agg', pairs + [(j, i) for i, j in pairs])]
    pallas_call x1, Pallas kernels: 6.4 us -> 4.93 us  [first_kernel(): pl.pallas_call(functools.partial(own_kernel, fr, ka, b, chunks), out_shap...]
    all_gather x1, blocking collectives: 17.5 us -> 16.6 us  [body(): whole = lax.all_gather(mine, 'grp', tiled=True, axis_index_groups=falling)]
  transfers between devices with their start and end apart: 2 -> 2, of which waited for: 1 -> 1; matrix products, arithmetic and copies ran while one was open for 0% -> 0% of each run, Pallas kernels for 10% -> 8%
where the time goes in v4:
time: 62.7 us; the launch traced here: 62.4 us
  blocking collectives  45.4 us (72%)
  starting transfers between devices  7.28 us (12%)
  Pallas kernels  5.63 us (9%)
  local copies, waits for them, and re-layouts  1.98 us (3%)
  waiting for transfers between devices  1.87 us (3%)
    all_to_all x1, blocking collectives, body(): lax.all_to_all(pair, 'grp', 0, 0, tiled=True, axis_index_groups=same_core)  24.9 us
    all_gather x1, blocking collectives, body(): whole = lax.all_gather(mine, 'grp', tiled=True, axis_index_groups=falling)  16.6 us
    ppermute x2, starting transfers between devices, swap(): return lax.ppermute(ends, 'agg', pairs + [(j, i) for i, j in pairs])  7.28 us
    pallas_call x1, Pallas kernels, first_kernel(): pl.pallas_call(functools.partial(own_kernel, fr, ka, b, chunks), out_shap...  4.93 us
    all_gather x1, blocking collectives, body(): sent = lax.all_gather(send, 'grp', axis_index_groups=chips)  3.93 us
    ppermute x2, waiting for transfers between devices, swap(): return lax.ppermute(ends, 'agg', pairs + [(j, i) for i, j in pairs])  1.87 us
  transfers between devices with their start and end apart: 2, of which 1 were waited for; matrix products, arithmetic and copies ran while one was open for 0% of the time, Pallas kernels for 8%

profile of v4, /device:TPU:7, one launch (start us, length us, event | category | flops | bytes accessed | tf_op | source)
XLA Modules:
  0.0 62.4 jit_solution(3224110158951980291)
XLA Ops:
  0.0 1.1 %dynamic-slice_bitcast_fusion = (bf16[4,2,128,128]{3,2,1,0:T(8,128)(2,1)S(1)}, bf16[4,2,128,128]{3,2,1,0:T(8,128)(2,1)S(1)}) fusion(bf16[1,1,16,2,128,128]{5,4,3,2,1,0:T(8,128)(2,1)} %param.6, s32[]{:T(128)S(6)} %select_n.11, s32[]{:T(128)S(6)} %select_n.10), kind=kLoop, calls=%fused_computation.2 | loop fusion | bytes 1048584 | tf_op jit(solution)/shard_map/dynamic_slice | solution.py:179
  1.1 5.4 %collective-permute-start.1 = (bf16[4,2,128,128]{3,2,1,0:T(8,128)(2,1)S(1)}, bf16[4,2,128,128]{3,2,1,0:T(8,128)(2,1)S(1)}, u32[]{:S(2)}, u32[]{:S(2)}) collective-permute-start(bf16[4,2,128,128]{3,2,1,0:T(8,128)(2,1)S(1)} %get-tuple-element.17), channel_id=1, source_target_pairs={{16,32},{48,64},{80,96},{112,128},{144,160},{176,192},{208,224},{2... | collective-permute-start | bytes 786440 | tf_op jit(solution)/shard_map/ppermute | solution.py:180
  6.4 1.9 %collective-permute-start = (bf16[4,2,128,128]{3,2,1,0:T(8,128)(2,1)S(1)}, bf16[4,2,128,128]{3,2,1,0:T(8,128)(2,1)S(1)}, u32[]{:S(2)}, u32[]{:S(2)}) collective-permute-start(bf16[4,2,128,128]{3,2,1,0:T(8,128)(2,1)S(1)} %get-tuple-element.18), channel_id=1, source_target_pairs={{0,16},{32,48},{64,80},{96,112},{128,144},{160,176},{192,208},{224... | collective-permute-start | bytes 786440 | tf_op jit(solution)/shard_map/ppermute | solution.py:180
  8.4 4.9 %own_part.1 = (bf16[384,384]{1,0:T(8,128)(2,1)S(1)}, bf16[384,512]{1,0:T(8,128)(2,1)S(1)}, bf16[384,512]{1,0:T(8,128)(2,1)S(1)}, bf16[2,4,2,3,16,128]{5,4,3,2,1,0:T(8,128)(2,1)S(1)}) custom-call(s32[5,1,16]{2,1,0:T(1,128)} %bitcast.26, s32[16,2,32]{2,1,0:T(2,128)} %bitcast.25, bf16[16,5,128,128]{3,2,1,0:T(8,128)(2,1)} %bitcast.24, ...), custom_call_target="tpu_custom_call" | custom-call | flops 2000000000 | bytes 6000000 | tf_op jit(solution)/shard_map/own_part/pallas_call | solution.py:142
  13.3 0.0 collective-permute-done.1.second
  13.3 1.9 %collective-permute-done.first = bf16[4,2,128,128]{3,2,1,0:T(8,128)(2,1)S(1)} collective-permute-done((bf16[4,2,128,128]{3,2,1,0:T(8,128)(2,1)S(1)}, bf16[4,2,128,128]{3,2,1,0:T(8,128)(2,1)S(1)}, u32[]{:S(2)}, u32[]{:S(2)}) %collective-permute-start) | collective-permute-done | bytes 262176 | tf_op jit(solution)/shard_map/ppermute | solution.py:180
  15.2 0.7 %halo_part.1 = (bf16[8,216,128]{2,1,0:T(8,128)(2,1)S(1)}, bf16[8,216,128]{2,1,0:T(8,128)(2,1)S(1)}) custom-call(bf16[384,384]{1,0:T(8,128)(2,1)S(1)} %get-tuple-element.11.own, bf16[384,512]{1,0:T(8,128)(2,1)S(1)} %get-tuple-element.12.v_first, bf16[384,512]{1,0:T(8,128)(2,1)S(1)} %get-tuple-element.13.v_second, ...), custom_call_target="tpu_custom_call" | custom-call | flops 400000000 | bytes 3000000 | tf_op jit(solution)/shard_map/halo_part/pallas_call | solution.py:187
  15.9 3.9 %all-gather = bf16[16,216,128]{2,1,0:T(8,128)(2,1)S(1)} all-gather(bf16[8,216,128]{2,1,0:T(8,128)(2,1)S(1)} %get-tuple-element.16), channel_id=2, replica_groups={{0,1},{2,3},{4,5},{6,7},{8,9},{10,11},{12,13},{14,15},{16,17},{18,19},{..., dimensions={0}, use_global_device_ids=true | all-gather | bytes 1327104 | tf_op jit(solution)/shard_map/all_gather | solution.py:200
  19.8 0.1 fusion
  19.9 24.9 %all_to_all.5 = bf16[8,216,128]{2,1,0:T(8,128)(2,1)S(1)} all-to-all(bf16[8,216,128]{2,1,0:T(8,128)(2,1)S(1)} %fusion), channel_id=1, replica_groups={{14,12,10,8,6,4,2,0},{1,3,5,7,9,11,13,15},{30,28,26,24,22,20,18,16},{17..., dimensions={0} | all-to-all | bytes 884736 | tf_op jit(solution)/shard_map/all_to_all | solution.py:204
  44.8 0.1 reduce_sum.12
  44.9 16.6 %all_gather.11 = bf16[3456,128]{1,0:T(8,128)(2,1)S(1)} all-gather(bf16[216,128]{1,0:T(8,128)(2,1)S(1)} %reduce_sum.12), channel_id=1, replica_groups={{14,15,12,13,10,11,8,9,6,7,4,5,2,3,0,1},{30,31,28,29,26,27,24,25,22,23,..., dimensions={0}, use_global_device_ids=true | all-gather | bytes 940032 | tf_op jit(solution)/shard_map/all_gather | solution.py:206
  61.5 0.9 %copy.6 = bf16[1,128,3,9,128]{4,1,3,2,0:T(8,128)(2,1)} copy(bf16[1,128,3,9,128]{4,1,3,2,0:T(8,128)(2,1)S(1)} %bitcast.21) | data formatting | bytes 1769472
Async XLA Ops:
  1.1 12.2 %collective-permute-start.1 = (bf16[4,2,128,128]{3,2,1,0:T(8,128)(2,1)S(1)}, bf16[4,2,128,128]{3,2,1,0:T(8,128)(2,1)S(1)}, u32[]{:S(2)}, u32[]{:S(2)}) collective-permute-start(bf16[4,2,128,128]{3,2,1,0:T(8,128)(2,1)S(1)} %get-tuple-element.17), channel_id=1, source_target_pairs={{16,32},{48,64},{80,96},{112,128},{144,160},{176,192},{208,224},{2... | collective-permute-start | bytes 786440 | tf_op jit(solution)/shard_map/ppermute | solution.py:180
  6.4 8.8 %collective-permute-start = (bf16[4,2,128,128]{3,2,1,0:T(8,128)(2,1)S(1)}, bf16[4,2,128,128]{3,2,1,0:T(8,128)(2,1)S(1)}, u32[]{:S(2)}, u32[]{:S(2)}) collective-permute-start(bf16[4,2,128,128]{3,2,1,0:T(8,128)(2,1)S(1)} %get-tuple-element.18), channel_id=1, source_target_pairs={{0,16},{32,48},{64,80},{96,112},{128,144},{160,176},{192,208},{224... | collective-permute-start | bytes 786440 | tf_op jit(solution)/shard_map/ppermute | solution.py:180

commit v5 on v4

--- a/solution.py
+++ b/solution.py
@@ -38,7 +38,7 @@
     copies[0].wait()
     mask[...] = jnp.zeros_like(mask)
     one = jnp.ones(mask.shape[-2:], BF16)
-    odd = lax.rem(region, 2)
+    odd = lax.rem(region + lax.axis_index("grp"), 2)
     for side in range(2):
         low = odd == 1 - side
         source = jnp.where(low, jnp.maximum(region - 1, 0), jnp.minimum(region + 1, last))
@@ -90,7 +90,7 @@
 
 def halo_kernel(b, pieces, own, v_first, v_second, mask, first, second, keep, send):
     core = lax.rem(lax.axis_index("grp"), 2)
-    odd = lax.rem(lax.axis_index("agg"), 2) == 1
+    odd = lax.rem(lax.axis_index("agg") + lax.axis_index("grp"), 2) == 1
     band = 3 * NC
     per = NC * band * b // pieces
     tile = mask.shape[-2]
@@ -172,12 +172,16 @@
     pieces = lax.axis_size("grp")
     z_count = pieces // 2
     per = NC * band * b // pieces
-    odd = lax.rem(lax.axis_index("agg"), 2)
+    odd = lax.rem(lax.axis_index("agg") + lax.axis_index("grp"), 2)
 
     def swap(least, start):
-        pairs = [(i, i + 1) for i in range(least, regions - 1, 2)]
+        pairs = [
+            (i * pieces + g, (i + 1) * pieces + g)
+            for g in range(pieces)
+            for i in range((least + g) % 2, regions - 1, 2)
+        ]
         ends = lax.dynamic_slice_in_dim(p_local, start * (fr - HB), HB, 0)
-        return lax.ppermute(ends, "agg", pairs + [(j, i) for i, j in pairs])
+        return lax.ppermute(ends, ("agg", "grp"), pairs + [(j, i) for i, j in pairs])
 
     first, second = swap(0, 1 - odd), swap(1, odd)
 

time: 62.7 us -> 61.3 us (0.978)
  waiting for transfers between devices: 1.87 us -> 0.01 us
  starting transfers between devices: 7.28 us -> 8.34 us
    ppermute x2, waiting for transfers between devices: 1.87 us -> 0.01 us  [swap(): lax.ppermute(ends, ('agg', 'grp'), pairs + [(j, i) for i, j in pairs])]
    ppermute x2, starting transfers between devices: 7.28 us -> 8.34 us  [swap(): lax.ppermute(ends, ('agg', 'grp'), pairs + [(j, i) for i, j in pairs])]
  transfers between devices with their start and end apart: 2 -> 2, of which waited for: 1 -> 0; matrix products, arithmetic and copies ran while one was open for 0% -> 0% of each run, Pallas kernels for 8% -> 8%
where the time goes in v5:
time: 61.3 us; the launch traced here: 61 us
  blocking collectives  44.8 us (73%)
  starting transfers between devices  8.34 us (14%)
  Pallas kernels  5.64 us (9%)
  local copies, waits for them, and re-layouts  1.98 us (3%)
    all_to_all x1, blocking collectives, body(): lax.all_to_all(pair, 'grp', 0, 0, tiled=True, axis_index_groups=same_core)  24.9 us
    all_gather x1, blocking collectives, body(): whole = lax.all_gather(mine, 'grp', tiled=True, axis_index_groups=falling)  16.6 us
    ppermute x2, starting transfers between devices, swap(): lax.ppermute(ends, ('agg', 'grp'), pairs + [(j, i) for i, j in pairs])  8.34 us
    pallas_call x1, Pallas kernels, first_kernel(): pl.pallas_call(functools.partial(own_kernel, fr, ka, b, chunks), out_shap...  4.93 us
    all_gather x1, blocking collectives, body(): sent = lax.all_gather(send, 'grp', axis_index_groups=chips)  3.32 us
  transfers between devices with their start and end apart: 2, of which 0 were waited for; matrix products, arithmetic and copies ran while one was open for 0% of the time, Pallas kernels for 8%

profile of v5, /device:TPU:7, one launch (start us, length us, event | category | flops | bytes accessed | tf_op | source)
XLA Modules:
  0.0 61.0 jit_solution(2856521105235331839)
XLA Ops:
  0.0 1.1 %dynamic-slice_bitcast_fusion = (bf16[4,2,128,128]{3,2,1,0:T(8,128)(2,1)S(1)}, bf16[4,2,128,128]{3,2,1,0:T(8,128)(2,1)S(1)}) fusion(bf16[1,1,16,2,128,128]{5,4,3,2,1,0:T(8,128)(2,1)} %param.6, s32[]{:T(128)S(6)} %select_n.11, s32[]{:T(128)S(6)} %select_n.10), kind=kLoop, calls=%fused_computation.2 | loop fusion | bytes 1048584 | tf_op jit(solution)/shard_map/dynamic_slice | solution.py:183
  1.1 3.2 %collective-permute-start.1 = (bf16[4,2,128,128]{3,2,1,0:T(8,128)(2,1)S(1)}, bf16[4,2,128,128]{3,2,1,0:T(8,128)(2,1)S(1)}, u32[]{:S(2)}, u32[]{:S(2)}) collective-permute-start(bf16[4,2,128,128]{3,2,1,0:T(8,128)(2,1)S(1)} %get-tuple-element.17), channel_id=1, source_target_pairs={{16,32},{48,64},{80,96},{112,128},{144,160},{176,192},{208,224},{2... | collective-permute-start | bytes 786440 | tf_op jit(solution)/shard_map/ppermute | solution.py:184
  4.3 5.1 %collective-permute-start = (bf16[4,2,128,128]{3,2,1,0:T(8,128)(2,1)S(1)}, bf16[4,2,128,128]{3,2,1,0:T(8,128)(2,1)S(1)}, u32[]{:S(2)}, u32[]{:S(2)}) collective-permute-start(bf16[4,2,128,128]{3,2,1,0:T(8,128)(2,1)S(1)} %get-tuple-element.18), channel_id=1, source_target_pairs={{0,16},{32,48},{64,80},{96,112},{128,144},{160,176},{192,208},{224... | collective-permute-start | bytes 786440 | tf_op jit(solution)/shard_map/ppermute | solution.py:184
  9.4 4.9 %own_part.1 = (bf16[384,384]{1,0:T(8,128)(2,1)S(1)}, bf16[384,512]{1,0:T(8,128)(2,1)S(1)}, bf16[384,512]{1,0:T(8,128)(2,1)S(1)}, bf16[2,4,2,3,16,128]{5,4,3,2,1,0:T(8,128)(2,1)S(1)}) custom-call(s32[5,1,16]{2,1,0:T(1,128)} %bitcast.26, s32[16,2,32]{2,1,0:T(2,128)} %bitcast.25, bf16[16,5,128,128]{3,2,1,0:T(8,128)(2,1)} %bitcast.24, ...), custom_call_target="tpu_custom_call" | custom-call | flops 2000000000 | bytes 6000000 | tf_op jit(solution)/shard_map/own_part/pallas_call | solution.py:142
  14.4 0.0 collective-permute-done.1.second
  14.4 0.0 collective-permute-done.first
  14.4 0.7 %halo_part.1 = (bf16[8,216,128]{2,1,0:T(8,128)(2,1)S(1)}, bf16[8,216,128]{2,1,0:T(8,128)(2,1)S(1)}) custom-call(bf16[384,384]{1,0:T(8,128)(2,1)S(1)} %get-tuple-element.11.own, bf16[384,512]{1,0:T(8,128)(2,1)S(1)} %get-tuple-element.12.v_first, bf16[384,512]{1,0:T(8,128)(2,1)S(1)} %get-tuple-element.13.v_second, ...), custom_call_target="tpu_custom_call" | custom-call | flops 400000000 | bytes 3000000 | tf_op jit(solution)/shard_map/halo_part/pallas_call | solution.py:191
  15.1 3.3 %all-gather = bf16[16,216,128]{2,1,0:T(8,128)(2,1)S(1)} all-gather(bf16[8,216,128]{2,1,0:T(8,128)(2,1)S(1)} %get-tuple-element.16), channel_id=2, replica_groups={{0,1},{2,3},{4,5},{6,7},{8,9},{10,11},{12,13},{14,15},{16,17},{18,19},{..., dimensions={0}, use_global_device_ids=true | all-gather | bytes 1327104 | tf_op jit(solution)/shard_map/all_gather | solution.py:204
  18.4 0.1 fusion
  18.5 24.9 %all_to_all.5 = bf16[8,216,128]{2,1,0:T(8,128)(2,1)S(1)} all-to-all(bf16[8,216,128]{2,1,0:T(8,128)(2,1)S(1)} %fusion), channel_id=1, replica_groups={{14,12,10,8,6,4,2,0},{1,3,5,7,9,11,13,15},{30,28,26,24,22,20,18,16},{17..., dimensions={0} | all-to-all | bytes 884736 | tf_op jit(solution)/shard_map/all_to_all | solution.py:208
  43.4 0.1 reduce_sum.12
  43.5 16.6 %all_gather.11 = bf16[3456,128]{1,0:T(8,128)(2,1)S(1)} all-gather(bf16[216,128]{1,0:T(8,128)(2,1)S(1)} %reduce_sum.12), channel_id=1, replica_groups={{14,15,12,13,10,11,8,9,6,7,4,5,2,3,0,1},{30,31,28,29,26,27,24,25,22,23,..., dimensions={0}, use_global_device_ids=true | all-gather | bytes 940032 | tf_op jit(solution)/shard_map/all_gather | solution.py:210
  60.1 0.9 %copy.6 = bf16[1,128,3,9,128]{4,1,3,2,0:T(8,128)(2,1)} copy(bf16[1,128,3,9,128]{4,1,3,2,0:T(8,128)(2,1)S(1)} %bitcast.21) | data formatting | bytes 1769472
Async XLA Ops:
  1.1 13.3 %collective-permute-start.1 = (bf16[4,2,128,128]{3,2,1,0:T(8,128)(2,1)S(1)}, bf16[4,2,128,128]{3,2,1,0:T(8,128)(2,1)S(1)}, u32[]{:S(2)}, u32[]{:S(2)}) collective-permute-start(bf16[4,2,128,128]{3,2,1,0:T(8,128)(2,1)S(1)} %get-tuple-element.17), channel_id=1, source_target_pairs={{16,32},{48,64},{80,96},{112,128},{144,160},{176,192},{208,224},{2... | collective-permute-start | bytes 786440 | tf_op jit(solution)/shard_map/ppermute | solution.py:184
  4.3 10.1 %collective-permute-start = (bf16[4,2,128,128]{3,2,1,0:T(8,128)(2,1)S(1)}, bf16[4,2,128,128]{3,2,1,0:T(8,128)(2,1)S(1)}, u32[]{:S(2)}, u32[]{:S(2)}) collective-permute-start(bf16[4,2,128,128]{3,2,1,0:T(8,128)(2,1)S(1)} %get-tuple-element.18), channel_id=1, source_target_pairs={{0,16},{32,48},{64,80},{96,112},{128,144},{160,176},{192,208},{224... | collective-permute-start | bytes 786440 | tf_op jit(solution)/shard_map/ppermute | solution.py:184

commit v6 on v5

--- a/solution.py
+++ b/solution.py
@@ -29,13 +29,15 @@
     for i in range(chunks):
         rows = pl.ds(i * step, step)
         copies.append(pltpu.make_async_copy(a_hbm.at[rows], a.at[rows], sems.at[3 + i]))
-    for copy in copies:
+    for copy in copies[: 3 + 1]:
         copy.start()
 
     zeros = jnp.zeros((b, b), BF16)
     for d in range(NC):
         routed[d, pl.ds(fr * b, b), :] = zeros
     copies[0].wait()
+    for copy in copies[3 + 1 :]:
+        copy.start()
     mask[...] = jnp.zeros_like(mask)
     one = jnp.ones(mask.shape[-2:], BF16)
     odd = lax.rem(region + lax.axis_index("grp"), 2)
@@ -135,7 +137,7 @@
     fr, ka, b = a_local.shape[:3]
     acol = a_cols[0].transpose(2, 0, 1)
     pcol = p_cols[:, 0].transpose(1, 2, 0)
-    chunks = 4
+    chunks = 2
     vmem = pl.BlockSpec(memory_space=pltpu.VMEM)
     hbm = pl.BlockSpec(memory_space=pltpu.HBM)
     n = NC * b

time: 61.3 us -> 61.3 us (level)
  no operation moved by 1% of the time
where the time goes in v6:
time: 61.3 us; the launch traced here: 61 us
  blocking collectives  44.9 us (73%)
  starting transfers between devices  8.34 us (14%)
  Pallas kernels  5.52 us (9%)
  local copies, waits for them, and re-layouts  1.98 us (3%)
    all_to_all x1, blocking collectives, body(): lax.all_to_all(pair, 'grp', 0, 0, tiled=True, axis_index_groups=same_core)  24.9 us
    all_gather x1, blocking collectives, body(): whole = lax.all_gather(mine, 'grp', tiled=True, axis_index_groups=falling)  16.6 us
    ppermute x2, starting transfers between devices, swap(): lax.ppermute(ends, ('agg', 'grp'), pairs + [(j, i) for i, j in pairs])  8.34 us
    pallas_call x1, Pallas kernels, first_kernel(): pl.pallas_call(functools.partial(own_kernel, fr, ka, b, chunks), out_shap...  4.82 us
    all_gather x1, blocking collectives, body(): sent = lax.all_gather(send, 'grp', axis_index_groups=chips)  3.43 us
  transfers between devices with their start and end apart: 2, of which 0 were waited for; matrix products, arithmetic and copies ran while one was open for 0% of the time, Pallas kernels for 8%

profile of v6, /device:TPU:7, one launch (start us, length us, event | category | flops | bytes accessed | tf_op | source)
XLA Modules:
  0.0 61.0 jit_solution(4041797279127450537)
XLA Ops:
  0.0 1.1 %dynamic-slice_bitcast_fusion = (bf16[4,2,128,128]{3,2,1,0:T(8,128)(2,1)S(1)}, bf16[4,2,128,128]{3,2,1,0:T(8,128)(2,1)S(1)}) fusion(bf16[1,1,16,2,128,128]{5,4,3,2,1,0:T(8,128)(2,1)} %param.6, s32[]{:T(128)S(6)} %select_n.11, s32[]{:T(128)S(6)} %select_n.10), kind=kLoop, calls=%fused_computation.2 | loop fusion | bytes 1048584 | tf_op jit(solution)/shard_map/dynamic_slice | solution.py:185
  1.1 3.2 %collective-permute-start.1 = (bf16[4,2,128,128]{3,2,1,0:T(8,128)(2,1)S(1)}, bf16[4,2,128,128]{3,2,1,0:T(8,128)(2,1)S(1)}, u32[]{:S(2)}, u32[]{:S(2)}) collective-permute-start(bf16[4,2,128,128]{3,2,1,0:T(8,128)(2,1)S(1)} %get-tuple-element.17), channel_id=1, source_target_pairs={{16,32},{48,64},{80,96},{112,128},{144,160},{176,192},{208,224},{2... | collective-permute-start | bytes 786440 | tf_op jit(solution)/shard_map/ppermute | solution.py:186
  4.3 5.1 %collective-permute-start = (bf16[4,2,128,128]{3,2,1,0:T(8,128)(2,1)S(1)}, bf16[4,2,128,128]{3,2,1,0:T(8,128)(2,1)S(1)}, u32[]{:S(2)}, u32[]{:S(2)}) collective-permute-start(bf16[4,2,128,128]{3,2,1,0:T(8,128)(2,1)S(1)} %get-tuple-element.18), channel_id=1, source_target_pairs={{0,16},{32,48},{64,80},{96,112},{128,144},{160,176},{192,208},{224... | collective-permute-start | bytes 786440 | tf_op jit(solution)/shard_map/ppermute | solution.py:186
  9.4 4.8 %own_part.1 = (bf16[384,384]{1,0:T(8,128)(2,1)S(1)}, bf16[384,512]{1,0:T(8,128)(2,1)S(1)}, bf16[384,512]{1,0:T(8,128)(2,1)S(1)}, bf16[2,4,2,3,16,128]{5,4,3,2,1,0:T(8,128)(2,1)S(1)}) custom-call(s32[5,1,16]{2,1,0:T(1,128)} %bitcast.26, s32[16,2,32]{2,1,0:T(2,128)} %bitcast.25, bf16[16,5,128,128]{3,2,1,0:T(8,128)(2,1)} %bitcast.24, ...), custom_call_target="tpu_custom_call" | custom-call | flops 2000000000 | bytes 6000000 | tf_op jit(solution)/shard_map/own_part/pallas_call | solution.py:144
  14.3 0.0 collective-permute-done.1.second
  14.3 0.0 collective-permute-done.first
  14.3 0.7 %halo_part.1 = (bf16[8,216,128]{2,1,0:T(8,128)(2,1)S(1)}, bf16[8,216,128]{2,1,0:T(8,128)(2,1)S(1)}) custom-call(bf16[384,384]{1,0:T(8,128)(2,1)S(1)} %get-tuple-element.11.own, bf16[384,512]{1,0:T(8,128)(2,1)S(1)} %get-tuple-element.12.v_first, bf16[384,512]{1,0:T(8,128)(2,1)S(1)} %get-tuple-element.13.v_second, ...), custom_call_target="tpu_custom_call" | custom-call | flops 400000000 | bytes 3000000 | tf_op jit(solution)/shard_map/halo_part/pallas_call | solution.py:193
  15.0 3.4 %all-gather = bf16[16,216,128]{2,1,0:T(8,128)(2,1)S(1)} all-gather(bf16[8,216,128]{2,1,0:T(8,128)(2,1)S(1)} %get-tuple-element.16), channel_id=2, replica_groups={{0,1},{2,3},{4,5},{6,7},{8,9},{10,11},{12,13},{14,15},{16,17},{18,19},{..., dimensions={0}, use_global_device_ids=true | all-gather | bytes 1327104 | tf_op jit(solution)/shard_map/all_gather | solution.py:206
  18.4 0.1 fusion
  18.5 24.9 %all_to_all.5 = bf16[8,216,128]{2,1,0:T(8,128)(2,1)S(1)} all-to-all(bf16[8,216,128]{2,1,0:T(8,128)(2,1)S(1)} %fusion), channel_id=1, replica_groups={{14,12,10,8,6,4,2,0},{1,3,5,7,9,11,13,15},{30,28,26,24,22,20,18,16},{17..., dimensions={0} | all-to-all | bytes 884736 | tf_op jit(solution)/shard_map/all_to_all | solution.py:210
  43.4 0.1 reduce_sum.12
  43.5 16.6 %all_gather.11 = bf16[3456,128]{1,0:T(8,128)(2,1)S(1)} all-gather(bf16[216,128]{1,0:T(8,128)(2,1)S(1)} %reduce_sum.12), channel_id=1, replica_groups={{14,15,12,13,10,11,8,9,6,7,4,5,2,3,0,1},{30,31,28,29,26,27,24,25,22,23,..., dimensions={0}, use_global_device_ids=true | all-gather | bytes 940032 | tf_op jit(solution)/shard_map/all_gather | solution.py:212
  60.1 0.9 %copy.6 = bf16[1,128,3,9,128]{4,1,3,2,0:T(8,128)(2,1)} copy(bf16[1,128,3,9,128]{4,1,3,2,0:T(8,128)(2,1)S(1)} %bitcast.21) | data formatting | bytes 1769472
Async XLA Ops:
  1.1 13.2 %collective-permute-start.1 = (bf16[4,2,128,128]{3,2,1,0:T(8,128)(2,1)S(1)}, bf16[4,2,128,128]{3,2,1,0:T(8,128)(2,1)S(1)}, u32[]{:S(2)}, u32[]{:S(2)}) collective-permute-start(bf16[4,2,128,128]{3,2,1,0:T(8,128)(2,1)S(1)} %get-tuple-element.17), channel_id=1, source_target_pairs={{16,32},{48,64},{80,96},{112,128},{144,160},{176,192},{208,224},{2... | collective-permute-start | bytes 786440 | tf_op jit(solution)/shard_map/ppermute | solution.py:186
  4.3 10.0 %collective-permute-start = (bf16[4,2,128,128]{3,2,1,0:T(8,128)(2,1)S(1)}, bf16[4,2,128,128]{3,2,1,0:T(8,128)(2,1)S(1)}, u32[]{:S(2)}, u32[]{:S(2)}) collective-permute-start(bf16[4,2,128,128]{3,2,1,0:T(8,128)(2,1)S(1)} %get-tuple-element.18), channel_id=1, source_target_pairs={{0,16},{32,48},{64,80},{96,112},{128,144},{160,176},{192,208},{224... | collective-permute-start | bytes 786440 | tf_op jit(solution)/shard_map/ppermute | solution.py:186

commit v7 on v6

--- a/solution.py
+++ b/solution.py
@@ -73,9 +73,6 @@
         right = jnp.concatenate([block_row(s) for s in starts], axis=0)
         g = jnp.dot(left, right, preferred_element_type=F32)
         grouped[pl.ds(r * b, b), :] = g.astype(BF16)
-    every = jnp.concatenate([routed[d, pl.ds(0, fr * b), :] for d in range(NC)], axis=1)
-    own[...] = contract_rows(every, grouped[...]).astype(BF16)
-
     for side, out in enumerate((v_first, v_second)):
         low = odd == 1 - side
         first_row, slot, base = jnp.where(low, 0, fr - HB), jnp.where(low, 1, ka - 1), jnp.where(low, 0, HB + fr)
@@ -88,6 +85,9 @@
         here = pl.ds(pl.multiple_of(first_row * b, b), HB * b)
         left = jnp.concatenate([routed[d, here, :] for d in range(NC)], axis=1)
         out[...] = contract_rows(left, jnp.concatenate(rows, axis=0)).astype(BF16)
+
+    every = jnp.concatenate([routed[d, pl.ds(0, fr * b), :] for d in range(NC)], axis=1)
+    own[...] = contract_rows(every, grouped[...]).astype(BF16)
 
 
 def halo_kernel(b, pieces, own, v_first, v_second, mask, first, second, keep, send):

time: 61.3 us -> 61.3 us (level)
  no operation moved by 1% of the time
where the time goes in v7:
time: 61.3 us; the launch traced here: 61 us
  blocking collectives  44.9 us (73%)
  starting transfers between devices  8.34 us (14%)
  Pallas kernels  5.54 us (9%)
  local copies, waits for them, and re-layouts  1.98 us (3%)
    all_to_all x1, blocking collectives, body(): lax.all_to_all(pair, 'grp', 0, 0, tiled=True, axis_index_groups=same_core)  24.9 us
    all_gather x1, blocking collectives, body(): whole = lax.all_gather(mine, 'grp', tiled=True, axis_index_groups=falling)  16.6 us
    ppermute x2, starting transfers between devices, swap(): lax.ppermute(ends, ('agg', 'grp'), pairs + [(j, i) for i, j in pairs])  8.34 us
    pallas_call x1, Pallas kernels, first_kernel(): pl.pallas_call(functools.partial(own_kernel, fr, ka, b, chunks), out_shap...  4.82 us
    all_gather x1, blocking collectives, body(): sent = lax.all_gather(send, 'grp', axis_index_groups=chips)  3.42 us
  transfers between devices with their start and end apart: 2, of which 0 were waited for; matrix products, arithmetic and copies ran while one was open for 0% of the time, Pallas kernels for 8%

profile of v7, /device:TPU:7, one launch (start us, length us, event | category | flops | bytes accessed | tf_op | source)
XLA Modules:
  0.0 61.0 jit_solution(3354357004985571133)
XLA Ops:
  0.0 1.1 %dynamic-slice_bitcast_fusion = (bf16[4,2,128,128]{3,2,1,0:T(8,128)(2,1)S(1)}, bf16[4,2,128,128]{3,2,1,0:T(8,128)(2,1)S(1)}) fusion(bf16[1,1,16,2,128,128]{5,4,3,2,1,0:T(8,128)(2,1)} %param.6, s32[]{:T(128)S(6)} %select_n.11, s32[]{:T(128)S(6)} %select_n.10), kind=kLoop, calls=%fused_computation.2 | loop fusion | bytes 1048584 | tf_op jit(solution)/shard_map/dynamic_slice | solution.py:185
  1.1 3.2 %collective-permute-start.1 = (bf16[4,2,128,128]{3,2,1,0:T(8,128)(2,1)S(1)}, bf16[4,2,128,128]{3,2,1,0:T(8,128)(2,1)S(1)}, u32[]{:S(2)}, u32[]{:S(2)}) collective-permute-start(bf16[4,2,128,128]{3,2,1,0:T(8,128)(2,1)S(1)} %get-tuple-element.17), channel_id=1, source_target_pairs={{16,32},{48,64},{80,96},{112,128},{144,160},{176,192},{208,224},{2... | collective-permute-start | bytes 786440 | tf_op jit(solution)/shard_map/ppermute | solution.py:186
  4.3 5.1 %collective-permute-start = (bf16[4,2,128,128]{3,2,1,0:T(8,128)(2,1)S(1)}, bf16[4,2,128,128]{3,2,1,0:T(8,128)(2,1)S(1)}, u32[]{:S(2)}, u32[]{:S(2)}) collective-permute-start(bf16[4,2,128,128]{3,2,1,0:T(8,128)(2,1)S(1)} %get-tuple-element.18), channel_id=1, source_target_pairs={{0,16},{32,48},{64,80},{96,112},{128,144},{160,176},{192,208},{224... | collective-permute-start | bytes 786440 | tf_op jit(solution)/shard_map/ppermute | solution.py:186
  9.4 4.8 %own_part.1 = (bf16[384,384]{1,0:T(8,128)(2,1)S(1)}, bf16[384,512]{1,0:T(8,128)(2,1)S(1)}, bf16[384,512]{1,0:T(8,128)(2,1)S(1)}, bf16[2,4,2,3,16,128]{5,4,3,2,1,0:T(8,128)(2,1)S(1)}) custom-call(s32[5,1,16]{2,1,0:T(1,128)} %bitcast.26, s32[16,2,32]{2,1,0:T(2,128)} %bitcast.25, bf16[16,5,128,128]{3,2,1,0:T(8,128)(2,1)} %bitcast.24, ...), custom_call_target="tpu_custom_call" | custom-call | flops 2000000000 | bytes 6000000 | tf_op jit(solution)/shard_map/own_part/pallas_call | solution.py:144
  14.3 0.0 collective-permute-done.1.second
  14.3 0.0 collective-permute-done.first
  14.3 0.7 %halo_part.1 = (bf16[8,216,128]{2,1,0:T(8,128)(2,1)S(1)}, bf16[8,216,128]{2,1,0:T(8,128)(2,1)S(1)}) custom-call(bf16[384,384]{1,0:T(8,128)(2,1)S(1)} %get-tuple-element.11.own, bf16[384,512]{1,0:T(8,128)(2,1)S(1)} %get-tuple-element.12.v_first, bf16[384,512]{1,0:T(8,128)(2,1)S(1)} %get-tuple-element.13.v_second, ...), custom_call_target="tpu_custom_call" | custom-call | flops 400000000 | bytes 3000000 | tf_op jit(solution)/shard_map/halo_part/pallas_call | solution.py:193
  15.0 3.4 %all-gather = bf16[16,216,128]{2,1,0:T(8,128)(2,1)S(1)} all-gather(bf16[8,216,128]{2,1,0:T(8,128)(2,1)S(1)} %get-tuple-element.16), channel_id=2, replica_groups={{0,1},{2,3},{4,5},{6,7},{8,9},{10,11},{12,13},{14,15},{16,17},{18,19},{..., dimensions={0}, use_global_device_ids=true | all-gather | bytes 1327104 | tf_op jit(solution)/shard_map/all_gather | solution.py:206
  18.4 0.1 fusion
  18.5 24.9 %all_to_all.5 = bf16[8,216,128]{2,1,0:T(8,128)(2,1)S(1)} all-to-all(bf16[8,216,128]{2,1,0:T(8,128)(2,1)S(1)} %fusion), channel_id=1, replica_groups={{14,12,10,8,6,4,2,0},{1,3,5,7,9,11,13,15},{30,28,26,24,22,20,18,16},{17..., dimensions={0} | all-to-all | bytes 884736 | tf_op jit(solution)/shard_map/all_to_all | solution.py:210
  43.4 0.1 reduce_sum.12
  43.5 16.6 %all_gather.11 = bf16[3456,128]{1,0:T(8,128)(2,1)S(1)} all-gather(bf16[216,128]{1,0:T(8,128)(2,1)S(1)} %reduce_sum.12), channel_id=1, replica_groups={{14,15,12,13,10,11,8,9,6,7,4,5,2,3,0,1},{30,31,28,29,26,27,24,25,22,23,..., dimensions={0}, use_global_device_ids=true | all-gather | bytes 940032 | tf_op jit(solution)/shard_map/all_gather | solution.py:212
  60.1 0.9 %copy.6 = bf16[1,128,3,9,128]{4,1,3,2,0:T(8,128)(2,1)} copy(bf16[1,128,3,9,128]{4,1,3,2,0:T(8,128)(2,1)S(1)} %bitcast.21) | data formatting | bytes 1769472
Async XLA Ops:
  1.1 13.2 %collective-permute-start.1 = (bf16[4,2,128,128]{3,2,1,0:T(8,128)(2,1)S(1)}, bf16[4,2,128,128]{3,2,1,0:T(8,128)(2,1)S(1)}, u32[]{:S(2)}, u32[]{:S(2)}) collective-permute-start(bf16[4,2,128,128]{3,2,1,0:T(8,128)(2,1)S(1)} %get-tuple-element.17), channel_id=1, source_target_pairs={{16,32},{48,64},{80,96},{112,128},{144,160},{176,192},{208,224},{2... | collective-permute-start | bytes 786440 | tf_op jit(solution)/shard_map/ppermute | solution.py:186
  4.3 10.0 %collective-permute-start = (bf16[4,2,128,128]{3,2,1,0:T(8,128)(2,1)S(1)}, bf16[4,2,128,128]{3,2,1,0:T(8,128)(2,1)S(1)}, u32[]{:S(2)}, u32[]{:S(2)}) collective-permute-start(bf16[4,2,128,128]{3,2,1,0:T(8,128)(2,1)S(1)} %get-tuple-element.18), channel_id=1, source_target_pairs={{0,16},{32,48},{64,80},{96,112},{128,144},{160,176},{192,208},{224... | collective-permute-start | bytes 786440 | tf_op jit(solution)/shard_map/ppermute | solution.py:186
